TPU v7x, 256 devices: a whole 4x4x8 slice. The times are simulated.
256 devices in a mesh: dp: 32 (over y, z), vocab: 8 (over x, core).
Axes of the slice: x: 4, y: 4, z: 8, core: 2. Of those that a mesh axis runs over, the one named last changes fastest.
Arguments:
- hidden: bfloat16 [24576, 2048], P('dp', 'vocab')
- gain: bfloat16 [2048], replicated, may hold values from 0.5 to 1.5
- head: bfloat16 [2048, 32000], P('dp', 'vocab')
- target_ids: int32 [24576], P('dp'), may hold values from 0 to 31999
- seq_lens: int32 [64], replicated, may hold values from 64 to 704, as said below
- seq_owner: int32 [64], replicated, may hold values from 0 to 31, as said below
Outputs:
- logprob: float32 [24576], P('dp')
- entropy: float32 [24576], P('dp')
Inputs may be any that keep to these rules, and one draw needn't show every extreme that they name: `seq_lens`: the lengths of the sequences owned by one dp index sum to at most 768; in every draw the sequences of some dp index sum to exactly 768. `seq_owner`: every dp index owns exactly 2 sequences.
All inputs are finite; a program needn't handle non-finite values.
Results may differ from a plain program's by a relative error of at most 0.0075.
Values may be sent and summed in bfloat16 or wider, within the bound.
A program may use at most 64 MiB of HBM per device.

v0:
```python
import jax
import jax.numpy as jnp
from jax import lax
from jax.sharding import PartitionSpec as P

EPS = 1e-05


def row_stats(normed, token_ids, columns, offset):
    count = normed.shape[0]
    width = normed.shape[1]
    block_rows = min(128, count)
    blocks = count // block_rows
    breadth = columns.shape[1]

    def compute(block_norm, block_ids):
        logits = jnp.dot(block_norm, columns, preferred_element_type=jnp.float32)
        top = jnp.max(logits, axis=1)
        expo = jnp.exp(logits - top[:, None])
        total = jnp.sum(expo, axis=1)
        weighted = jnp.sum(expo * logits, axis=1)
        local_id = block_ids - offset
        matches = jnp.arange(breadth, dtype=jnp.int32)[None, :] == local_id[:, None]
        picked = jnp.sum(jnp.where(matches, logits, 0.0), axis=1)
        return (top, total, weighted, picked)

    def per_block(item):
        block_norm, block_ids, start = item
        return compute(block_norm, block_ids)

    starts = jnp.arange(blocks, dtype=jnp.int32) * block_rows
    result = lax.map(
        per_block,
        (normed.reshape(blocks, block_rows, width), token_ids.reshape(blocks, block_rows), starts),
    )
    return tuple((member.reshape(count) for member in result))


def local(hidden, gain, head, target_ids, seq_lens, seq_owner):
    groups = lax.axis_size("dp")
    position = lax.axis_index("dp")
    slice_index = lax.axis_index("vocab")
    slots = hidden.shape[0]
    breadth = head.shape[1]
    owners = jnp.arange(groups, dtype=jnp.int32)
    loads = jnp.sum(jnp.where(seq_owner[:, None] == owners[None, :], seq_lens[:, None], 0), axis=0)
    own_live = jnp.arange(slots, dtype=jnp.int32) < loads[position]
    features = lax.all_gather(hidden, "vocab", axis=1, tiled=True)
    wide = features.astype(jnp.float32)
    normed = (
        wide
        * lax.rsqrt(jnp.mean(wide * wide, axis=1, keepdims=True) + EPS)
        * gain.astype(jnp.float32)
    ).astype(jnp.bfloat16)
    columns = lax.all_gather(head, "dp", axis=0, tiled=True)
    stats = row_stats(normed, target_ids, columns, slice_index * breadth)
    top = lax.pmax(stats[0], "vocab")
    factor = jnp.exp(stats[0] - top)
    total, weighted, picked = lax.psum((stats[1] * factor, stats[2] * factor, stats[3]), "vocab")
    lse = top + jnp.log(total)
    logprob = picked - lse
    entropy = lse - weighted / total
    return (jnp.where(own_live, logprob, 0.0), jnp.where(own_live, entropy, 0.0))


def solution(mesh):
    return jax.shard_map(
        local,
        mesh=mesh,
        in_specs=(P("dp", "vocab"), P(), P("dp", "vocab"), P("dp"), P(), P()),
        out_specs=(P("dp"), P("dp")),
        check_vma=False,
    )
```

profile of v0, /device:TPU:1, one launch (start us, length us, event | category | flops | bytes accessed | tf_op | source)
XLA Modules:
  0.0 305.6 jit_solution(14415921997200401669)
XLA Ops:
  7.2 0.0 all-gather.3.cloned.1.call-start
  7.2 0.7 all-gather.3.cloned.1.call-update
  7.9 0.0 all-gather.5.cloned.1.call-start
  7.9 0.7 all-gather.5.cloned.1.call-update
  8.7 0.7 convert_element_type.10
  9.4 0.8 select_reduce_fusion.1
  10.2 0.6 dynamic_slice.11
  10.8 37.5 %all-gather.3.cloned.1.call-done = bf16[768,2048]{1,0:T(8,128)(2,1)} async-done(((bf16[768,256]{1,0:T(8,128)(2,1)}), bf16[768,2048]{1,0:T(8,128)(2,1)}) %all-gather.3.cloned.1.call-update) | async-done | bytes 3145744 | tf_op jit(solution)/shard_map/all_gather | solution.py:48
  48.3 0.0 copy-start
  48.3 2.7 fusion.5
  51.0 0.1 copy-done
  51.1 2.5 fusion.7
  53.5 138.2 %all-gather.5.cloned.1.call-done = bf16[2048,4000]{1,0:T(8,128)(2,1)} async-done(((bf16[64,4000]{1,0:T(8,128)(2,1)}), bf16[2048,4000]{1,0:T(8,128)(2,1)}) %all-gather.5.cloned.1.call-update) | async-done | bytes 16384016 | tf_op jit(solution)/shard_map/all_gather | solution.py:55
  191.7 70.6 %while.16 = (s32[]{:T(128)}, f32[6,128]{1,0:T(8,128)S(1)}, f32[6,128]{1,0:T(8,128)S(1)}, f32[6,128]{1,0:T(8,128)S(1)}, f32[6,128]{1,0:T(8,128)S(1)}, /*index=5*/...) while((s32[]{:T(128)}, f32[6,128]{1,0:T(8,128)S(1)}, ...), condition=%wide.region_7.8_spmd, body=%wide.region_2.7_spmd.sunk | while | flops 2101247616 | bytes 21406340 | solution.py:32
  191.7 10.2 %fusion.13 = (f32[128]{0:T(128)S(1)}, f32[128,4000]{0,1:T(8,128)S(1)}) fusion(bf16[2048,4000]{1,0:T(8,128)(2,1)} %get-tuple-element.179, bf16[6,128,2048]{2,1,0:T(8,128)(2,1)} %get-tuple-element.178, s32[]{:T(128)} %get-tuple-element.162), kind=kOutput, calls=%fused_computation.25.clone.1 | convolution fusion | flops 2097663872 | bytes 19350528 | tf_op jit(solution)/shard_map/while/body/eval_jaxpr/dot_general | solution.py:17
  201.9 0.7 subtract_bitcast_fusion.2
  202.6 0.7 multiply_reduce_fusion.2
  203.5 10.2 %fusion.13 = (f32[128]{0:T(128)S(1)}, f32[128,4000]{0,1:T(8,128)S(1)}) fusion(bf16[2048,4000]{1,0:T(8,128)(2,1)} %get-tuple-element.179, bf16[6,128,2048]{2,1,0:T(8,128)(2,1)} %get-tuple-element.178, s32[]{:T(128)} %get-tuple-element.162), kind=kOutput, calls=%fused_computation.25.clone.1 | convolution fusion | flops 2097663872 | bytes 19350528 | tf_op jit(solution)/shard_map/while/body/eval_jaxpr/dot_general | solution.py:17
  213.7 0.7 subtract_bitcast_fusion.2
  214.4 0.7 multiply_reduce_fusion.2
  215.2 10.2 %fusion.13 = (f32[128]{0:T(128)S(1)}, f32[128,4000]{0,1:T(8,128)S(1)}) fusion(bf16[2048,4000]{1,0:T(8,128)(2,1)} %get-tuple-element.179, bf16[6,128,2048]{2,1,0:T(8,128)(2,1)} %get-tuple-element.178, s32[]{:T(128)} %get-tuple-element.162), kind=kOutput, calls=%fused_computation.25.clone.1 | convolution fusion | flops 2097663872 | bytes 19350528 | tf_op jit(solution)/shard_map/while/body/eval_jaxpr/dot_general | solution.py:17
  225.5 0.7 subtract_bitcast_fusion.2
  226.2 0.7 multiply_reduce_fusion.2
  227.0 10.2 %fusion.13 = (f32[128]{0:T(128)S(1)}, f32[128,4000]{0,1:T(8,128)S(1)}) fusion(bf16[2048,4000]{1,0:T(8,128)(2,1)} %get-tuple-element.179, bf16[6,128,2048]{2,1,0:T(8,128)(2,1)} %get-tuple-element.178, s32[]{:T(128)} %get-tuple-element.162), kind=kOutput, calls=%fused_computation.25.clone.1 | convolution fusion | flops 2097663872 | bytes 19350528 | tf_op jit(solution)/shard_map/while/body/eval_jaxpr/dot_general | solution.py:17
  237.2 0.7 subtract_bitcast_fusion.2
  237.9 0.7 multiply_reduce_fusion.2
  238.8 10.2 %fusion.13 = (f32[128]{0:T(128)S(1)}, f32[128,4000]{0,1:T(8,128)S(1)}) fusion(bf16[2048,4000]{1,0:T(8,128)(2,1)} %get-tuple-element.179, bf16[6,128,2048]{2,1,0:T(8,128)(2,1)} %get-tuple-element.178, s32[]{:T(128)} %get-tuple-element.162), kind=kOutput, calls=%fused_computation.25.clone.1 | convolution fusion | flops 2097663872 | bytes 19350528 | tf_op jit(solution)/shard_map/while/body/eval_jaxpr/dot_general | solution.py:17
  249.0 0.7 subtract_bitcast_fusion.2
  249.7 0.7 multiply_reduce_fusion.2
  250.6 10.2 %fusion.13 = (f32[128]{0:T(128)S(1)}, f32[128,4000]{0,1:T(8,128)S(1)}) fusion(bf16[2048,4000]{1,0:T(8,128)(2,1)} %get-tuple-element.179, bf16[6,128,2048]{2,1,0:T(8,128)(2,1)} %get-tuple-element.178, s32[]{:T(128)} %get-tuple-element.162), kind=kOutput, calls=%fused_computation.25.clone.1 | convolution fusion | flops 2097663872 | bytes 19350528 | tf_op jit(solution)/shard_map/while/body/eval_jaxpr/dot_general | solution.py:17
  260.8 0.7 subtract_bitcast_fusion.2
  261.5 0.7 multiply_reduce_fusion.2
  262.3 12.8 %pmax.7 = f32[768]{0:T(1024)S(1)} all-reduce(f32[768]{0:T(1024)S(1)} %bitcast.42), channel_id=1, replica_groups=mesh['dp'=32,'vocab'=8] {'vocab'}, use_global_device_ids=true, to_apply=%region_9.10 | all-reduce | flops 768 | bytes 6144 | tf_op jit(solution)/shard_map/pmax | solution.py:57
  275.2 22.4 %all-reduce = (f32[768]{0:T(1024)S(1)}, f32[768]{0:T(1024)S(1)}, f32[768]{0:T(1024)S(1)}) all-reduce(f32[768]{0:T(1024)S(1)} %bitcast.43, f32[768]{0:T(1024)S(1)} %get-tuple-element.85, f32[768]{0:T(1024)S(1)} %get-tuple-element.84), channel_id=1, replica_groups=mesh['dp'=32,'vocab'=8] {'vocab'}, use_global_device_ids=true, to_apply=%region_8.9 | all-reduce | flops 2304 | bytes 18432 | tf_op jit(solution)/shard_map/psum | solution.py:59
  297.6 1.2 subtract_select_fusion
  (30 shorter events, 0.8 us)
Async XLA Ops:
  7.2 41.1 %all-gather.3.cloned.1.call-start = ((), (), s32[]{:S(2)}) async-start(), calls=%async_computation | async-start | bytes 3538944 | tf_op jit(solution)/shard_map/all_gather | solution.py:48
  7.9 183.8 %all-gather.5.cloned.1.call-start = ((), (), s32[]{:S(2)}) async-start(), calls=%async_computation.1 | async-start | bytes 17301504 | tf_op jit(solution)/shard_map/all_gather | solution.py:55
  48.3 2.8 copy-start
Sparse Core Ops, SparseCore 0:
  9.8 38.3 all-gather.2
  50.8 140.8 all-gather.4
where the time goes:
time: 307 us; the launch traced here: 306 us
  waiting for transfers between devices  177 us (58%)
  matrix products  61.4 us (20%)
  blocking collectives  35.2 us (11%)
  other arithmetic  16.2 us (5%)
  between operations  14.1 us (5%)
    all_gather x1, waiting for transfers between devices, local(): columns = lax.all_gather(head, 'dp', axis=0, tiled=True)  138 us
    dot_general x6, matrix products, compute(): logits = jnp.dot(block_norm, columns, preferred_element_type=jnp.float32)  61.4 us
    all_gather x1, waiting for transfers between devices, local(): features = lax.all_gather(hidden, 'vocab', axis=1, tiled=True)  37.5 us
    psum x1, blocking collectives, local(): lax.psum((stats[1] * factor, stats[2] * factor, stats[3]), 'vocab')  22.4 us
    pmax x1, blocking collectives, local(): top = lax.pmax(stats[0], 'vocab')  12.8 us
  transfers between devices with their start and end apart: 2, of which 2 were waited for; matrix products, arithmetic and copies ran while one was open for 2% of the time, Pallas kernels for 0%

commit v1 on v0

v1 whole, which is shorter than its diff:
```python
import jax
import jax.numpy as jnp
from jax import lax
from jax.sharding import PartitionSpec as P

EPS = 1e-05


def chunk_bounds(breadth, parts):
    step = -(-breadth // parts)
    step = -(-step // 128) * 128
    bounds = []
    start = 0
    while start < breadth:
        stop = min(start + step, breadth)
        bounds.append((start, stop))
        start = stop
    return bounds


def chunk_stats(normed, columns, local_id, start):
    logits = jnp.dot(normed, columns, preferred_element_type=jnp.float32)
    top = jnp.max(logits, axis=1)
    expo = jnp.exp(logits - top[:, None])
    total = jnp.sum(expo, axis=1)
    weighted = jnp.sum(expo * logits, axis=1)
    ids = start + lax.broadcasted_iota(jnp.int32, logits.shape, 1)
    picked = jnp.sum(jnp.where(ids == local_id[:, None], logits, 0.0), axis=1)
    return top, total, weighted, picked


def local(hidden, gain, head, target_ids, seq_lens, seq_owner):
    groups = lax.axis_size("dp")
    position = lax.axis_index("dp")
    slice_index = lax.axis_index("vocab")
    slots = hidden.shape[0]
    breadth = head.shape[1]
    owners = jnp.arange(groups, dtype=jnp.int32)
    loads = jnp.sum(jnp.where(seq_owner[:, None] == owners[None, :], seq_lens[:, None], 0), axis=0)
    own_live = jnp.arange(slots, dtype=jnp.int32) < loads[position]
    features = lax.all_gather(hidden, "vocab", axis=1, tiled=True)
    wide = features.astype(jnp.float32)
    normed = (
        wide
        * lax.rsqrt(jnp.mean(wide * wide, axis=1, keepdims=True) + EPS)
        * gain.astype(jnp.float32)
    ).astype(jnp.bfloat16)
    local_id = target_ids - slice_index * breadth
    parts = []
    for start, stop in chunk_bounds(breadth, 4):
        columns = lax.all_gather(head[:, start:stop], "dp", axis=0, tiled=True)
        parts.append(chunk_stats(normed, columns, local_id, start))
    tops = jnp.stack([p[0] for p in parts])
    top_local = jnp.max(tops, axis=0)
    scale = jnp.exp(tops - top_local[None, :])
    total_local = jnp.sum(jnp.stack([p[1] for p in parts]) * scale, axis=0)
    weighted_local = jnp.sum(jnp.stack([p[2] for p in parts]) * scale, axis=0)
    picked_local = jnp.sum(jnp.stack([p[3] for p in parts]), axis=0)
    top = lax.pmax(top_local, "vocab")
    factor = jnp.exp(top_local - top)
    total, weighted, picked = lax.psum(
        (total_local * factor, weighted_local * factor, picked_local), "vocab"
    )
    lse = top + jnp.log(total)
    logprob = picked - lse
    entropy = lse - weighted / total
    return (jnp.where(own_live, logprob, 0.0), jnp.where(own_live, entropy, 0.0))


def solution(mesh):
    return jax.shard_map(
        local,
        mesh=mesh,
        in_specs=(P("dp", "vocab"), P(), P("dp", "vocab"), P("dp"), P(), P()),
        out_specs=(P("dp"), P("dp")),
        check_vma=False,
    )
```

time: 307 us -> 432 us (1.41)
  waiting for transfers between devices: 177 us -> 337 us
  matrix products: 61.4 us -> 27.2 us
  other arithmetic: 16.2 us -> 11.6 us
    all_gather x1 -> x4, waiting for transfers between devices: 138 us -> 303 us  [local(): columns = lax.all_gather(head[:, start:stop], 'dp', axis=0, tiled=True)]
    dot_general x6 -> x4, matrix products: 61.4 us -> 27.2 us  [chunk_stats(): logits = jnp.dot(normed, columns, preferred_element_type=jnp.float32)]
    all_gather x1, waiting for transfers between devices: 37.5 us -> 32.8 us  [local(): features = lax.all_gather(hidden, 'vocab', axis=1, tiled=True)]
  transfers between devices with their start and end apart: 2 -> 5, of which waited for: 2 -> 5; matrix products, arithmetic and copies ran while one was open for 2% -> 7% of each run, Pallas kernels for 0% -> 0%
where the time goes in v1:
time: 432 us; the launch traced here: 430 us
  waiting for transfers between devices  337 us (78%)
  blocking collectives  35.8 us (8%)
  matrix products  27.2 us (6%)
  between operations  13.9 us (3%)
  other arithmetic  11.6 us (3%)
    all_gather x4, waiting for transfers between devices, local(): columns = lax.all_gather(head[:, start:stop], 'dp', axis=0, tiled=True)  303 us
    all_gather x1, waiting for transfers between devices, local(): features = lax.all_gather(hidden, 'vocab', axis=1, tiled=True)  32.8 us
    dot_general x4, matrix products, chunk_stats(): logits = jnp.dot(normed, columns, preferred_element_type=jnp.float32)  27.2 us
    psum x1, blocking collectives, local(): lax.psum((total_local * factor, weighted_local * factor, picked_local), '...  20.7 us
    pmax x1, blocking collectives, local(): top = lax.pmax(top_local, 'vocab')  15.1 us
  transfers between devices with their start and end apart: 5, of which 5 were waited for; matrix products, arithmetic and copies ran while one was open for 7% of the time, Pallas kernels for 0%

profile of v1, /device:TPU:1, one launch (start us, length us, event | category | flops | bytes accessed | tf_op | source)
XLA Modules:
  0.0 430.1 jit_solution(7421292452426967437)
XLA Ops:
  7.2 0.0 all-gather.6.cloned.1.call-start
  7.2 0.7 all-gather.6.cloned.1.call-update
  7.9 0.0 all-gather.14.cloned.1.call-start
  7.9 1.6 slice.15
  9.5 0.0 all-gather.14.cloned.1.call-update
  9.5 0.0 all-gather.8.cloned.1.call-start
  9.6 1.8 fusion.20
  11.4 0.0 all-gather.8.cloned.1.call-update
  11.4 0.0 all-gather.10.cloned.1.call-start
  11.5 0.5 all-gather.10.cloned.1.call-update
  12.0 0.0 all-gather.12.cloned.1.call-start
  12.0 0.5 all-gather.12.cloned.1.call-update
  12.6 0.7 convert_element_type.10
  13.3 0.8 select_reduce_fusion.4
  14.1 0.7 dynamic_slice.3
  14.7 0.7 broadcast_subtract_fusion
  15.4 32.8 %all-gather.6.cloned.1.call-done = bf16[768,2048]{1,0:T(8,128)(2,1)} async-done(((bf16[768,256]{1,0:T(8,128)(2,1)}), bf16[768,2048]{1,0:T(8,128)(2,1)}) %all-gather.6.cloned.1.call-update) | async-done | bytes 3145744 | tf_op jit(solution)/shard_map/all_gather | solution.py:41
  48.3 0.0 copy-start.1
  48.3 2.7 fusion
  51.0 79.6 %all-gather.14.cloned.1.call-done = bf16[2048,928]{1,0:T(8,128)(2,1)} async-done(((bf16[64,928]{1,0:T(8,128)(2,1)}), bf16[2048,928]{1,0:T(8,128)(2,1)}) %all-gather.14.cloned.1.call-update) | async-done | bytes 3801104 | tf_op jit(solution)/shard_map/all_gather | solution.py:51
  130.6 0.0 copy-done.1
  130.6 5.9 %fusion.21 = (f32[768]{0:T(1024)S(1)}, f32[768,928]{0,1:T(8,128)S(1)}) fusion(bf16[2048,928]{1,0:T(8,128)(2,1)} %all-gather.14.cloned.1.call-done, bf16[768,2048]{1,0:T(8,128)(2,1)S(1)} %copy-done.1, f32[2048]{0:T(1024)S(1)} %convert_element_type.10, f32[768]{0:T(1024)S(1)} %add_rsqrt_fusion), kind=kOutput, calls=%fused_computation.49 | convolution fusion | flops 2926238976 | bytes 9811968 | tf_op jit(solution)/shard_map/dot_general | solution.py:22
  136.5 0.9 multiply_reduce_fusion.3
  137.4 74.9 %all-gather.8.cloned.1.call-done = bf16[2048,1024]{1,0:T(8,128)(2,1)} async-done(((bf16[64,1024]{1,0:T(8,128)(2,1)}), bf16[2048,1024]{1,0:T(8,128)(2,1)}) %all-gather.8.cloned.1.call-update) | async-done | bytes 4194320 | tf_op jit(solution)/shard_map/all_gather | solution.py:51
  212.3 6.4 %fusion.24 = (f32[768]{0:T(1024)S(1)}, f32[768,1024]{1,0:T(8,128)S(1)}) fusion(bf16[2048,1024]{1,0:T(8,128)(2,1)} %all-gather.8.cloned.1.call-done, bf16[768,2048]{1,0:T(8,128)(2,1)} %all-gather.6.cloned.1.call-done, f32[2048]{0:T(1024)S(1)} %convert_element_type.10, f32[768]{0:T(1024)S(1)} %add_rsqrt_fusion), kind=kOutput, calls=%fused_computation.52 | convolution fusion | flops 3228302592 | bytes 10500096 | tf_op jit(solution)/shard_map/dot_general | solution.py:22
  218.7 75.1 %all-gather.10.cloned.1.call-done = bf16[2048,1024]{1,0:T(8,128)(2,1)} async-done(((bf16[64,1024]{1,0:T(8,128)(2,1)}), bf16[2048,1024]{1,0:T(8,128)(2,1)}) %all-gather.10.cloned.1.call-update) | async-done | bytes 4194320 | tf_op jit(solution)/shard_map/all_gather | solution.py:51
  293.8 8.4 %fusion.22 = (f32[768]{0:T(1024)S(1)}, f32[768,1024]{1,0:T(8,128)}) fusion(bf16[2048,1024]{1,0:T(8,128)(2,1)} %all-gather.10.cloned.1.call-done, bf16[768,2048]{1,0:T(8,128)(2,1)} %all-gather.6.cloned.1.call-done, f32[2048]{0:T(1024)S(1)} %convert_element_type.10, f32[768]{0:T(1024)S(1)} %add_rsqrt_fusion), kind=kOutput, calls=%fused_computation.50 | convolution fusion | flops 3228302592 | bytes 10500096 | tf_op jit(solution)/shard_map/dot_general | solution.py:22
  302.2 73.2 %all-gather.12.cloned.1.call-done = bf16[2048,1024]{1,0:T(8,128)(2,1)} async-done(((bf16[64,1024]{1,0:T(8,128)(2,1)}), bf16[2048,1024]{1,0:T(8,128)(2,1)}) %all-gather.12.cloned.1.call-update) | async-done | bytes 4194320 | tf_op jit(solution)/shard_map/all_gather | solution.py:51
  375.4 0.0 copy-start
  375.4 6.6 %fusion.23 = (f32[768]{0:T(1024)S(1)}, f32[768,1024]{1,0:T(8,128)S(1)}) fusion(bf16[2048,1024]{1,0:T(8,128)(2,1)} %all-gather.12.cloned.1.call-done, bf16[768,2048]{1,0:T(8,128)(2,1)} %all-gather.6.cloned.1.call-done, f32[2048]{0:T(1024)S(1)} %convert_element_type.10, f32[768]{0:T(1024)S(1)} %add_rsqrt_fusion), kind=kOutput, calls=%fused_computation.51 | convolution fusion | flops 3228302592 | bytes 10500096 | tf_op jit(solution)/shard_map/dot_general | solution.py:22
  382.0 0.0 copy-done
  382.0 4.4 %multiply_reduce_fusion.1 = (f32[768]{0:T(1024)S(1)}, f32[768]{0:T(1024)S(1)}, f32[768]{0:T(1024)S(1)}, f32[768]{0:T(1024)S(1)}, f32[768]{0:T(1024)S(1)}, /*inde...) fusion(f32[768,1024]{1,0:T(8,128)S(1)} %copy-done, f32[768]{0:T(1024)S(1)} %get-tuple-element.34, ...), kind=kLoop, calls=%fused_computation.6 | loop fusion | flops 16508160 | bytes 9485312 | tf_op jit(solution)/shard_map/reduce_sum | solution.py:26
  386.5 15.1 %pmax.7 = f32[768]{0:T(1024)S(1)} all-reduce(f32[768]{0:T(1024)S(1)} %maximum_maximum_fusion), channel_id=1, replica_groups=mesh['dp'=32,'vocab'=8] {'vocab'}, use_global_device_ids=true, to_apply=%region_11.12 | all-reduce | flops 768 | bytes 6144 | tf_op jit(solution)/shard_map/pmax | solution.py:59
  401.6 0.1 fusion.9
  401.6 20.7 %all-reduce = (f32[768]{0:T(1024)S(1)}, f32[768]{0:T(1024)S(1)}, f32[768]{0:T(1024)S(1)}) all-reduce(f32[768]{0:T(1024)S(1)} %add_add_fusion, f32[768]{0:T(1024)S(1)} %get-tuple-element.25, f32[768]{0:T(1024)S(1)} %get-tuple-element.24), channel_id=1, replica_groups=mesh['dp'=32,'vocab'=8] {'vocab'}, use_global_device_ids=true, to_apply=%region_6.7 | all-reduce | flops 2304 | bytes 18432 | tf_op jit(solution)/shard_map/psum | solution.py:61
  422.3 1.3 subtract_select_fusion
  (18 shorter events, 0.1 us)
Async XLA Ops:
  7.2 41.1 %all-gather.6.cloned.1.call-start = ((), (), s32[]{:S(2)}) async-start(), calls=%async_computation | async-start | bytes 3538944 | tf_op jit(solution)/shard_map/all_gather | solution.py:41
  7.9 122.7 %all-gather.14.cloned.1.call-start = ((), (), s32[]{:S(2)}) async-start(), calls=%async_computation.4 | async-start | bytes 4325376 | tf_op jit(solution)/shard_map/all_gather | solution.py:51
  9.5 202.8 %all-gather.8.cloned.1.call-start = ((), (), s32[]{:S(2)}) async-start(), calls=%async_computation.1 | async-start | bytes 4325376 | tf_op jit(solution)/shard_map/all_gather | solution.py:51
  11.4 282.4 %all-gather.10.cloned.1.call-start = ((), (), s32[]{:S(2)}) async-start(), calls=%async_computation.2 | async-start | bytes 4325376 | tf_op jit(solution)/shard_map/all_gather | solution.py:51
  12.0 363.4 %all-gather.12.cloned.1.call-start = ((), (), s32[]{:S(2)}) async-start(), calls=%async_computation.3 | async-start | bytes 4325376 | tf_op jit(solution)/shard_map/all_gather | solution.py:51
  48.3 82.4 %copy-start.1 = (bf16[768,2048]{1,0:T(8,128)(2,1)S(1)}, bf16[768,2048]{1,0:T(8,128)(2,1)}, u32[]{:S(2)}) copy-start(bf16[768,2048]{1,0:T(8,128)(2,1)} %all-gather.6.cloned.1.call-done) | copy-start | bytes 9437188
  375.4 6.6 %copy-start = (f32[768,1024]{1,0:T(8,128)S(1)}, f32[768,1024]{1,0:T(8,128)}, u32[]{:S(2)}) copy-start(f32[768,1024]{1,0:T(8,128)} %get-tuple-element.35) | copy-start | bytes 9437188
Sparse Core Ops, SparseCore 0:
  9.8 38.3 all-gather.5
  50.8 79.7 all-gather.13
  133.2 79.0 all-gather.7
  214.8 79.0 all-gather.9
  296.3 79.0 all-gather.11

commit v2 on v0

v2 whole, which is shorter than its diff:
```python
import functools

import jax
import jax.numpy as jnp
from jax import lax
from jax.experimental import pallas as pl
from jax.experimental.pallas import tpu as pltpu
from jax.sharding import PartitionSpec as P

EPS = 1e-05
MESH = pl.DeviceIdType.MESH


def dp_grid(mesh):
    size = mesh.shape["dp"]
    try:
        zs = {tuple(mesh.devices[i, 0].coords)[2] for i in range(size)}
        nz = len(zs)
    except Exception:
        nz = size // 4
    return size // nz, nz


def head_gather_kernel(ny, nz, head_ref, out_ref, send_sem, recv_sem, local_sem):
    dp = lax.axis_index("dp")
    v = lax.axis_index("vocab")
    y = dp // nz
    z = dp % nz
    yr = (y + 1) % ny
    yl = (y + ny - 1) % ny

    def zs(k):
        return (z + k + 8 * nz) % nz

    def ys(k):
        return (y + k + 8 * ny) % ny

    def dev(yy, zz):
        return (yy * nz + zz, v)

    rows = head_ref.shape[1]
    hr = rows // 2

    barrier = pltpu.get_barrier_semaphore()
    peers = [dev(yr, z), dev(yl, z), dev(y, zs(1)), dev(y, zs(-1))]
    for peer in peers:
        pl.semaphore_signal(barrier, inc=1, device_id=peer, device_id_type=MESH)
    pl.semaphore_wait(barrier, len(peers))

    copies = {}

    def send(key, src, dst, peer):
        c = pltpu.make_async_remote_copy(
            src_ref=src,
            dst_ref=dst,
            send_sem=send_sem.at[len(copies)],
            recv_sem=recv_sem.at[len(copies)],
            device_id=peer,
            device_id_type=MESH,
        )
        copies[key] = c
        c.start()

    def arrived(key):
        copies[key].wait_recv()

    local = pltpu.make_async_copy(head_ref, out_ref.at[y, z], local_sem)
    local.start()

    send("ay_r1", head_ref.at[0], out_ref.at[y, z, 0], dev(yr, z))
    send("ay_l1", head_ref.at[0], out_ref.at[y, z, 0], dev(yl, z))
    send("bz_r1", head_ref.at[1], out_ref.at[y, z, 1], dev(y, zs(1)))
    send("bz_l1", head_ref.at[1], out_ref.at[y, z, 1], dev(y, zs(-1)))

    zhalf = nz // 2
    yhalf = ny // 2

    def fwd_single_z(step):
        src_r = zs(-(step - 1))
        src_l = zs(step - 1)
        if step < zhalf or nz % 2 == 1:
            send(f"bz_r{step}", out_ref.at[y, src_r, 1], out_ref.at[y, src_r, 1], dev(y, zs(1)))
            send(f"bz_l{step}", out_ref.at[y, src_l, 1], out_ref.at[y, src_l, 1], dev(y, zs(-1)))
        else:
            send(f"bz_r{step}", out_ref.at[y, src_r, 1, pl.ds(0, hr)],
                 out_ref.at[y, src_r, 1, pl.ds(0, hr)], dev(y, zs(1)))
            send(f"bz_l{step}", out_ref.at[y, src_l, 1, pl.ds(hr, hr)],
                 out_ref.at[y, src_l, 1, pl.ds(hr, hr)], dev(y, zs(-1)))

    def fwd_single_y(step):
        src_r = ys(-(step - 1))
        src_l = ys(step - 1)
        if step < yhalf or ny % 2 == 1:
            send(f"ay_r{step}", out_ref.at[src_r, z, 0], out_ref.at[src_r, z, 0], dev(yr, z))
            send(f"ay_l{step}", out_ref.at[src_l, z, 0], out_ref.at[src_l, z, 0], dev(yl, z))
        else:
            send(f"ay_r{step}", out_ref.at[src_r, z, 0, pl.ds(0, hr)],
                 out_ref.at[src_r, z, 0, pl.ds(0, hr)], dev(yr, z))
            send(f"ay_l{step}", out_ref.at[src_l, z, 0, pl.ds(hr, hr)],
                 out_ref.at[src_l, z, 0, pl.ds(hr, hr)], dev(yl, z))

    def fwd_group_z(step):
        src_r = zs(-(step - 1))
        src_l = zs(step - 1)
        if step < zhalf or nz % 2 == 1:
            send(f"az_r{step}", out_ref.at[:, src_r, 0], out_ref.at[:, src_r, 0], dev(y, zs(1)))
            send(f"az_l{step}", out_ref.at[:, src_l, 0], out_ref.at[:, src_l, 0], dev(y, zs(-1)))
        else:
            send(f"az_r{step}", out_ref.at[pl.ds(0, yhalf), src_r, 0],
                 out_ref.at[pl.ds(0, yhalf), src_r, 0], dev(y, zs(1)))
            send(f"az_l{step}", out_ref.at[pl.ds(yhalf, ny - yhalf), src_l, 0],
                 out_ref.at[pl.ds(yhalf, ny - yhalf), src_l, 0], dev(y, zs(-1)))

    def fwd_group_y(step):
        src_r = ys(-(step - 1))
        src_l = ys(step - 1)
        if step < yhalf or ny % 2 == 1:
            send(f"by_r{step}", out_ref.at[src_r, :, 1], out_ref.at[src_r, :, 1], dev(yr, z))
            send(f"by_l{step}", out_ref.at[src_l, :, 1], out_ref.at[src_l, :, 1], dev(yl, z))
        else:
            send(f"by_r{step}", out_ref.at[src_r, pl.ds(0, zhalf), 1],
                 out_ref.at[src_r, pl.ds(0, zhalf), 1], dev(yr, z))
            send(f"by_l{step}", out_ref.at[src_l, pl.ds(zhalf, nz - zhalf), 1],
                 out_ref.at[src_l, pl.ds(zhalf, nz - zhalf), 1], dev(yl, z))

    ysteps = ny // 2 if ny % 2 == 0 else (ny - 1) // 2
    zsteps = nz // 2 if nz % 2 == 0 else (nz - 1) // 2

    for step in range(2, max(ysteps, zsteps) + 1):
        if step <= ysteps:
            arrived(f"ay_r{step - 1}")
            arrived(f"ay_l{step - 1}")
            fwd_single_y(step)
        if step <= zsteps:
            arrived(f"bz_r{step - 1}")
            arrived(f"bz_l{step - 1}")
            fwd_single_z(step)
    local.wait()
    if ysteps >= 1:
        arrived(f"ay_r{ysteps}")
        arrived(f"ay_l{ysteps}")
    send("az_r1", out_ref.at[:, z, 0], out_ref.at[:, z, 0], dev(y, zs(1)))
    send("az_l1", out_ref.at[:, z, 0], out_ref.at[:, z, 0], dev(y, zs(-1)))
    if zsteps >= 1:
        arrived(f"bz_r{zsteps}")
        arrived(f"bz_l{zsteps}")
    send("by_r1", out_ref.at[y, :, 1], out_ref.at[y, :, 1], dev(yr, z))
    send("by_l1", out_ref.at[y, :, 1], out_ref.at[y, :, 1], dev(yl, z))
    for step in range(2, max(ysteps, zsteps) + 1):
        if step <= zsteps:
            arrived(f"az_r{step - 1}")
            arrived(f"az_l{step - 1}")
            fwd_group_z(step)
        if step <= ysteps:
            arrived(f"by_r{step - 1}")
            arrived(f"by_l{step - 1}")
            fwd_group_y(step)
    arrived(f"az_r{zsteps}")
    arrived(f"az_l{zsteps}")
    arrived(f"by_r{ysteps}")
    arrived(f"by_l{ysteps}")
    for c in copies.values():
        c.wait_send()


def gather_head(head, ny, nz):
    rows, width = head.shape
    blocks = head.reshape(2, rows // 2, width)
    streams = 4 * (ny // 2 + nz // 2)
    out = pl.pallas_call(
        functools.partial(head_gather_kernel, ny, nz),
        out_shape=jax.ShapeDtypeStruct((ny, nz, 2, rows // 2, width), head.dtype),
        in_specs=[pl.BlockSpec(memory_space=pl.ANY)],
        out_specs=pl.BlockSpec(memory_space=pl.ANY),
        scratch_shapes=[
            pltpu.SemaphoreType.DMA((streams,)),
            pltpu.SemaphoreType.DMA((streams,)),
            pltpu.SemaphoreType.DMA(()),
        ],
        compiler_params=pltpu.CompilerParams(collective_id=0, has_side_effects=True),
        cost_estimate=pl.CostEstimate(
            flops=0, transcendentals=0, bytes_accessed=2 * ny * nz * rows * width * 2
        ),
    )(blocks)
    return out.reshape(ny * nz * rows, width)


def stats_kernel(n, stats_ref, out_ref, send_sem, recv_sem):
    dp = lax.axis_index("dp")
    v = lax.axis_index("vocab")
    barrier = pltpu.get_barrier_semaphore()
    for k in range(1, n):
        pl.semaphore_signal(barrier, inc=1, device_id=(dp, (v + k) % n), device_id_type=MESH)
    pl.semaphore_wait(barrier, n - 1)
    copies = []
    for k in range(1, n):
        c = pltpu.make_async_remote_copy(
            src_ref=stats_ref,
            dst_ref=out_ref.at[v],
            send_sem=send_sem.at[k - 1],
            recv_sem=recv_sem.at[k - 1],
            device_id=(dp, (v + k) % n),
            device_id_type=MESH,
        )
        c.start()
        copies.append(c)
    out_ref[v] = stats_ref[...]
    for c in copies:
        c.wait_recv()
    for c in copies:
        c.wait_send()


def exchange_stats(stats, n):
    return pl.pallas_call(
        functools.partial(stats_kernel, n),
        out_shape=jax.ShapeDtypeStruct((n,) + stats.shape, stats.dtype),
        in_specs=[pl.BlockSpec(memory_space=pltpu.VMEM)],
        out_specs=pl.BlockSpec(memory_space=pltpu.VMEM),
        scratch_shapes=[
            pltpu.SemaphoreType.DMA((n - 1,)),
            pltpu.SemaphoreType.DMA((n - 1,)),
        ],
        compiler_params=pltpu.CompilerParams(collective_id=1, has_side_effects=True),
    )(stats)


def local(ny, nz, hidden, gain, head, target_ids, seq_lens, seq_owner):
    groups = lax.axis_size("dp")
    slices = lax.axis_size("vocab")
    position = lax.axis_index("dp")
    slice_index = lax.axis_index("vocab")
    slots = hidden.shape[0]
    breadth = head.shape[1]
    owners = jnp.arange(groups, dtype=jnp.int32)
    loads = jnp.sum(jnp.where(seq_owner[:, None] == owners[None, :], seq_lens[:, None], 0), axis=0)
    own_live = jnp.arange(slots, dtype=jnp.int32) < loads[position]
    columns = gather_head(head, ny, nz)
    features = lax.all_gather(hidden, "vocab", axis=1, tiled=True)
    wide = features.astype(jnp.float32)
    normed = (
        wide
        * lax.rsqrt(jnp.mean(wide * wide, axis=1, keepdims=True) + EPS)
        * gain.astype(jnp.float32)
    ).astype(jnp.bfloat16)
    logits = jnp.dot(normed, columns, preferred_element_type=jnp.float32)
    top_local = jnp.max(logits, axis=1)
    expo = jnp.exp(logits - top_local[:, None])
    total_local = jnp.sum(expo, axis=1)
    weighted_local = jnp.sum(expo * logits, axis=1)
    local_id = target_ids - slice_index * breadth
    ids = lax.broadcasted_iota(jnp.int32, logits.shape, 1)
    picked_local = jnp.sum(jnp.where(ids == local_id[:, None], logits, 0.0), axis=1)
    stats = jnp.stack([top_local, total_local, weighted_local, picked_local])
    every = exchange_stats(stats, slices)
    tops = every[:, 0]
    top = jnp.max(tops, axis=0)
    factor = jnp.exp(tops - top[None, :])
    total = jnp.sum(every[:, 1] * factor, axis=0)
    weighted = jnp.sum(every[:, 2] * factor, axis=0)
    picked = jnp.sum(every[:, 3], axis=0)
    lse = top + jnp.log(total)
    logprob = picked - lse
    entropy = lse - weighted / total
    return (jnp.where(own_live, logprob, 0.0), jnp.where(own_live, entropy, 0.0))


def solution(mesh):
    ny, nz = dp_grid(mesh)
    return jax.shard_map(
        functools.partial(local, ny, nz),
        mesh=mesh,
        in_specs=(P("dp", "vocab"), P(), P("dp", "vocab"), P("dp"), P(), P()),
        out_specs=(P("dp"), P("dp")),
        check_vma=False,
    )
```

time: 307 us -> 172 us (0.56)
  waiting for transfers between devices: 177 us -> 0.68 us
  Pallas kernels: 0 us -> 122 us
  matrix products: 61.4 us -> 20.9 us
  blocking collectives: 35.2 us -> 0 us
  other arithmetic: 16.2 us -> 12.8 us
    all_gather x1 -> x0, waiting for transfers between devices: 138 us -> none  [local(): columns = lax.all_gather(head, 'dp', axis=0, tiled=True)]
    pallas_call x0 -> x2, Pallas kernels: none -> 122 us  [the longest x1 107 us: gather_head(): pl.pallas_call(functools.partial(head_gather_kernel, ny, nz), out_shape=j...]
    dot_general x6 -> x1, matrix products: 61.4 us -> 20.9 us  [local(): logits = jnp.dot(normed, columns, preferred_element_type=jnp.float32)]
    all_gather x1, waiting for transfers between devices: 37.5 us -> 0.01 us  [local(): features = lax.all_gather(hidden, 'vocab', axis=1, tiled=True)]
    psum x1 -> x0, blocking collectives: 22.4 us -> none  [local(): lax.psum((stats[1] * factor, stats[2] * factor, stats[3]), 'vocab')]
    pmax x1 -> x0, blocking collectives: 12.8 us -> none  [local(): top = lax.pmax(stats[0], 'vocab')]
    sub x6 -> x1, other arithmetic: 4.2 us -> 0.01 us  [local(): local_id = target_ids - slice_index * breadth]
    reduce_sum x6 -> x2, other arithmetic: 4.09 us -> 7.01 us  [the longest x1 6.98 us: local(): total_local = jnp.sum(expo, axis=1)]
  transfers between devices with their start and end apart: 2 -> 1, of which waited for: 2 -> 0; matrix products, arithmetic and copies ran while one was open for 2% -> 0% of each run, Pallas kernels for 0% -> 62%
where the time goes in v2:
time: 172 us; the launch traced here: 171 us
  Pallas kernels  122 us (71%)
  matrix products  20.9 us (12%)
  between operations  14.2 us (8%)
  other arithmetic  12.8 us (7%)
    pallas_call x1, Pallas kernels, gather_head(): pl.pallas_call(functools.partial(head_gather_kernel, ny, nz), out_shape=j...  107 us
    dot_general x1, matrix products, local(): logits = jnp.dot(normed, columns, preferred_element_type=jnp.float32)  20.9 us
    pallas_call x1, Pallas kernels, exchange_stats(): pl.pallas_call(functools.partial(stats_kernel, n), out_shape=jax.ShapeDty...  15.4 us
    reduce_sum x1, other arithmetic, local(): total_local = jnp.sum(expo, axis=1)  6.98 us
  transfers between devices with their start and end apart: 1, of which 0 were waited for; matrix products, arithmetic and copies ran while one was open for 0% of the time, Pallas kernels for 62%

profile of v2, /device:TPU:1, one launch (start us, length us, event | category | flops | bytes accessed | tf_op | source)
XLA Modules:
  0.0 171.4 jit_solution(10840476364352497803)
XLA Ops:
  7.2 0.0 copy-start
  7.2 0.0 copy-start.2
  7.2 0.0 copy-start.3
  7.2 0.0 copy-start.1
  7.2 0.0 all-gather.2.cloned.1.call-start
  7.3 0.7 all-gather.2.cloned.1.call-update
  7.9 106.9 %shard_map.77 = bf16[4,8,2,32,4000]{4,3,2,1,0:T(8,128)(2,1)} custom-call(bf16[2,32,4000]{2,1,0:T(8,128)(2,1)} %bitcast.25), custom_call_target="tpu_custom_call" | custom-call | bytes 32768000 | tf_op jit(solution)/shard_map/pallas_call | solution.py:170
  114.8 0.0 copy-done
  114.9 0.0 copy-done.2
  114.9 0.0 copy-done.3
  114.9 0.1 select_reduce_fusion.1
  115.0 0.6 dynamic_slice.3
  115.6 0.0 copy-done.1
  115.6 0.0 all-gather.2.cloned.1.call-done
  115.6 2.6 %fusion.1 = f32[768]{0:T(1024)S(1)} fusion(bf16[768,2048]{1,0:T(8,128)(2,1)} %all-gather.2.cloned.1.call-done), kind=kLoop, calls=%fused_computation.7 | loop fusion | flops 4717824 | bytes 3148800 | tf_op jit(solution)/shard_map/reduce_sum | solution.py:243
  118.2 20.9 %fusion.14 = (f32[768]{0:T(1024)S(1)}, f32[768,4000]{0,1:T(8,128)}) fusion(bf16[2048,4000]{1,0:T(8,128)(2,1)} %bitcast.24, bf16[768,2048]{1,0:T(8,128)(2,1)} %all-gather.2.cloned.1.call-done, f32[2048]{0:T(1024)S(1)} %convert_element_type.10, f32[768]{0:T(1024)S(1)} %add_rsqrt_fusion), kind=kOutput, calls=%fused_computation.33 | convolution fusion | flops 12592274432 | bytes 31832064 | tf_op jit(solution)/shard_map/dot_general | solution.py:246
  139.1 7.0 %fusion = (f32[768]{0:T(1024)S(1)}, f32[768]{0:T(1024)S(1)}, f32[768]{0:T(1024)S(1)}) fusion(f32[768,4000]{0,1:T(8,128)} %get-tuple-element.17, f32[768]{0:T(1024)S(1)} %get-tuple-element.16, s32[768]{0:T(1024)S(1)} %broadcast_subtract_fusion), kind=kLoop, calls=%fused_computation.4 | loop fusion | flops 21501696 | bytes 12303360 | tf_op jit(solution)/shard_map/reduce_sum | solution.py:249
  146.2 0.6 pad_maximum_fusion.stats_ref
  146.8 15.4 %shard_map.78 = f32[8,4,768]{2,1,0:T(4,128)} custom-call(f32[4,768]{1,0:T(4,128)} %pad_maximum_fusion.stats_ref), custom_call_target="tpu_custom_call" | custom-call | tf_op jit(solution)/shard_map/pallas_call | solution.py:215
  162.1 1.2 fusion.13
  163.4 1.2 subtract_select_fusion
  (8 shorter events, 0.1 us)
Async XLA Ops:
  7.2 107.7 %copy-start = (bf16[2048]{0:T(1024)(128)(2,1)S(1)}, bf16[2048]{0:T(1024)(128)(2,1)}, u32[]{:S(2)}) copy-start(bf16[2048]{0:T(1024)(128)(2,1)} %param.7) | copy-start | bytes 12292
  7.2 107.7 %copy-start.2 = (s32[64]{0:T(128)S(1)}, s32[64]{0:T(128)}, u32[]{:S(2)}) copy-start(s32[64]{0:T(128)} %param.10) | copy-start | bytes 772
  7.2 107.7 %copy-start.3 = (s32[64]{0:T(128)S(1)}, s32[64]{0:T(128)}, u32[]{:S(2)}) copy-start(s32[64]{0:T(128)} %param.11) | copy-start | bytes 772
  7.2 108.4 %copy-start.1 = (s32[768]{0:T(1024)S(1)}, s32[768]{0:T(1024)}, u32[]{:S(2)}) copy-start(s32[768]{0:T(1024)} %param.9) | copy-start | bytes 9220
  7.2 108.4 %all-gather.2.cloned.1.call-start = ((), (), s32[]{:S(2)}) async-start(), calls=%async_computation | async-start | bytes 3538944 | tf_op jit(solution)/shard_map/all_gather | solution.py:239
Sparse Core Ops, SparseCore 0:
  9.9 38.3 all-gather.1

commit v3 on v2

v3 whole, which is shorter than its diff:
```python
import functools

import jax
import jax.numpy as jnp
from jax import lax
from jax.experimental import pallas as pl
from jax.experimental.pallas import tpu as pltpu
from jax.sharding import PartitionSpec as P

EPS = 1e-05
MESH = pl.DeviceIdType.MESH


def dp_grid(mesh):
    size = mesh.shape["dp"]
    try:
        zs = {tuple(mesh.devices[i, 0].coords)[2] for i in range(size)}
        nz = len(zs)
    except Exception:
        nz = size // 4
    return size // nz, nz


def head_gather_kernel(ny, nz, split, head_ref, out_ref, send_sem, recv_sem, local_sem):
    dp = lax.axis_index("dp")
    v = lax.axis_index("vocab")
    y = dp // nz
    z = dp % nz
    rows, width = head_ref.shape
    hr = rows // 2
    cols = (pl.ds(0, split), pl.ds(split, width - split))

    def zs(k):
        return (z + k + 8 * nz) % nz

    def ys(k):
        return (y + k + 8 * ny) % ny

    def dev(yy, zz):
        return (yy * nz + zz, v)

    right_y, left_y = dev(ys(1), z), dev(ys(-1), z)
    right_z, left_z = dev(y, zs(1)), dev(y, zs(-1))

    barrier = pltpu.get_barrier_semaphore()
    peers = [right_y, left_y, right_z, left_z]
    for peer in peers:
        pl.semaphore_signal(barrier, inc=1, device_id=peer, device_id_type=MESH)
    pl.semaphore_wait(barrier, len(peers))

    copies = {}

    def send(key, view, peer, src=None):
        c = pltpu.make_async_remote_copy(
            src_ref=view if src is None else src,
            dst_ref=view,
            send_sem=send_sem.at[len(copies)],
            recv_sem=recv_sem.at[len(copies)],
            device_id=peer,
            device_id_type=MESH,
        )
        copies[key] = c
        c.start()

    def arrived(key):
        copies[key].wait_recv()

    local = pltpu.make_async_copy(head_ref, out_ref.at[y, z], local_sem)
    local.start()

    ysteps = ny // 2
    zsteps = nz // 2

    def single_y(step):
        if step == 1:
            send("ay_r1", out_ref.at[y, z, :, cols[0]], right_y, head_ref.at[:, cols[0]])
            send("ay_l1", out_ref.at[y, z, :, cols[0]], left_y, head_ref.at[:, cols[0]])
            return
        src_r, src_l = ys(-(step - 1)), ys(step - 1)
        if step < ny - step or ny % 2 == 1:
            send(f"ay_r{step}", out_ref.at[src_r, z, :, cols[0]], right_y)
            send(f"ay_l{step}", out_ref.at[src_l, z, :, cols[0]], left_y)
        else:
            send(f"ay_r{step}", out_ref.at[src_r, z, pl.ds(0, hr), cols[0]], right_y)
            send(f"ay_l{step}", out_ref.at[src_l, z, pl.ds(hr, rows - hr), cols[0]], left_y)

    def single_z(step):
        if step == 1:
            send("bz_r1", out_ref.at[y, z, :, cols[1]], right_z, head_ref.at[:, cols[1]])
            send("bz_l1", out_ref.at[y, z, :, cols[1]], left_z, head_ref.at[:, cols[1]])
            return
        src_r, src_l = zs(-(step - 1)), zs(step - 1)
        if step < nz - step or nz % 2 == 1:
            send(f"bz_r{step}", out_ref.at[y, src_r, :, cols[1]], right_z)
            send(f"bz_l{step}", out_ref.at[y, src_l, :, cols[1]], left_z)
        else:
            send(f"bz_r{step}", out_ref.at[y, src_r, pl.ds(0, hr), cols[1]], right_z)
            send(f"bz_l{step}", out_ref.at[y, src_l, pl.ds(hr, rows - hr), cols[1]], left_z)

    def group_z(step):
        src_r, src_l = zs(-(step - 1)), zs(step - 1)
        if step < nz - step or nz % 2 == 1:
            send(f"az_r{step}", out_ref.at[:, src_r, :, cols[0]], right_z)
            send(f"az_l{step}", out_ref.at[:, src_l, :, cols[0]], left_z)
        else:
            half = ny // 2
            send(f"az_r{step}", out_ref.at[pl.ds(0, half), src_r, :, cols[0]], right_z)
            send(f"az_l{step}", out_ref.at[pl.ds(half, ny - half), src_l, :, cols[0]], left_z)

    def group_y(step):
        src_r, src_l = ys(-(step - 1)), ys(step - 1)
        if step < ny - step or ny % 2 == 1:
            send(f"by_r{step}", out_ref.at[src_r, :, :, cols[1]], right_y)
            send(f"by_l{step}", out_ref.at[src_l, :, :, cols[1]], left_y)
        else:
            half = nz // 2
            send(f"by_r{step}", out_ref.at[src_r, pl.ds(0, half), :, cols[1]], right_y)
            send(f"by_l{step}", out_ref.at[src_l, pl.ds(half, nz - half), :, cols[1]], left_y)

    single_y(1)
    single_z(1)
    for step in range(2, max(ysteps, zsteps) + 1):
        if step <= ysteps:
            arrived(f"ay_r{step - 1}")
            arrived(f"ay_l{step - 1}")
            single_y(step)
        if step <= zsteps:
            arrived(f"bz_r{step - 1}")
            arrived(f"bz_l{step - 1}")
            single_z(step)
    local.wait()
    arrived(f"ay_r{ysteps}")
    arrived(f"ay_l{ysteps}")
    send("az_r1", out_ref.at[:, z, :, cols[0]], right_z)
    send("az_l1", out_ref.at[:, z, :, cols[0]], left_z)
    arrived(f"bz_r{zsteps}")
    arrived(f"bz_l{zsteps}")
    send("by_r1", out_ref.at[y, :, :, cols[1]], right_y)
    send("by_l1", out_ref.at[y, :, :, cols[1]], left_y)
    for step in range(2, max(ysteps, zsteps) + 1):
        if step <= zsteps:
            arrived(f"az_r{step - 1}")
            arrived(f"az_l{step - 1}")
            group_z(step)
        if step <= ysteps:
            arrived(f"by_r{step - 1}")
            arrived(f"by_l{step - 1}")
            group_y(step)
    arrived(f"az_r{zsteps}")
    arrived(f"az_l{zsteps}")
    arrived(f"by_r{ysteps}")
    arrived(f"by_l{ysteps}")
    for c in copies.values():
        c.wait_send()


def gather_head(head, ny, nz):
    rows, width = head.shape
    share = 0.405
    split = max(128, min(width - 128, int(round(width * share / 128)) * 128))
    streams = 4 * (ny // 2 + nz // 2)
    out = pl.pallas_call(
        functools.partial(head_gather_kernel, ny, nz, split),
        out_shape=jax.ShapeDtypeStruct((ny, nz, rows, width), head.dtype),
        in_specs=[pl.BlockSpec(memory_space=pl.ANY)],
        out_specs=pl.BlockSpec(memory_space=pl.ANY),
        scratch_shapes=[
            pltpu.SemaphoreType.DMA((streams,)),
            pltpu.SemaphoreType.DMA((streams,)),
            pltpu.SemaphoreType.DMA(()),
        ],
        compiler_params=pltpu.CompilerParams(collective_id=0, has_side_effects=True),
        cost_estimate=pl.CostEstimate(
            flops=0, transcendentals=0, bytes_accessed=2 * ny * nz * rows * width * 2
        ),
    )(head)
    return out.reshape(ny * nz * rows, width)


def stats_kernel(n, stats_ref, out_ref, send_sem, recv_sem):
    dp = lax.axis_index("dp")
    v = lax.axis_index("vocab")
    barrier = pltpu.get_barrier_semaphore()
    for k in range(1, n):
        pl.semaphore_signal(barrier, inc=1, device_id=(dp, (v + k) % n), device_id_type=MESH)
    pl.semaphore_wait(barrier, n - 1)
    copies = []
    for k in range(1, n):
        c = pltpu.make_async_remote_copy(
            src_ref=stats_ref,
            dst_ref=out_ref.at[v],
            send_sem=send_sem.at[k - 1],
            recv_sem=recv_sem.at[k - 1],
            device_id=(dp, (v + k) % n),
            device_id_type=MESH,
        )
        c.start()
        copies.append(c)
    out_ref[v] = stats_ref[...]
    for c in copies:
        c.wait_recv()
    for c in copies:
        c.wait_send()


def exchange_stats(stats, n):
    return pl.pallas_call(
        functools.partial(stats_kernel, n),
        out_shape=jax.ShapeDtypeStruct((n,) + stats.shape, stats.dtype),
        in_specs=[pl.BlockSpec(memory_space=pltpu.VMEM)],
        out_specs=pl.BlockSpec(memory_space=pltpu.VMEM),
        scratch_shapes=[
            pltpu.SemaphoreType.DMA((n - 1,)),
            pltpu.SemaphoreType.DMA((n - 1,)),
        ],
        compiler_params=pltpu.CompilerParams(collective_id=1, has_side_effects=True),
    )(stats)


def local(ny, nz, hidden, gain, head, target_ids, seq_lens, seq_owner):
    groups = lax.axis_size("dp")
    slices = lax.axis_size("vocab")
    position = lax.axis_index("dp")
    slice_index = lax.axis_index("vocab")
    slots = hidden.shape[0]
    breadth = head.shape[1]
    owners = jnp.arange(groups, dtype=jnp.int32)
    loads = jnp.sum(jnp.where(seq_owner[:, None] == owners[None, :], seq_lens[:, None], 0), axis=0)
    own_live = jnp.arange(slots, dtype=jnp.int32) < loads[position]
    columns = gather_head(head, ny, nz)
    features = lax.all_gather(hidden, "vocab", axis=1, tiled=True)
    wide = features.astype(jnp.float32)
    normed = (
        wide
        * lax.rsqrt(jnp.mean(wide * wide, axis=1, keepdims=True) + EPS)
        * gain.astype(jnp.float32)
    ).astype(jnp.bfloat16)
    logits = jnp.dot(normed, columns, preferred_element_type=jnp.float32)
    top_local = jnp.max(logits, axis=1)
    expo = jnp.exp(logits - top_local[:, None])
    total_local = jnp.sum(expo, axis=1)
    weighted_local = jnp.sum(expo * logits, axis=1)
    local_id = target_ids - slice_index * breadth
    ids = lax.broadcasted_iota(jnp.int32, logits.shape, 1)
    picked_local = jnp.sum(jnp.where(ids == local_id[:, None], logits, 0.0), axis=1)
    stats = jnp.stack([top_local, total_local, weighted_local, picked_local])
    every = exchange_stats(stats, slices)
    tops = every[:, 0]
    top = jnp.max(tops, axis=0)
    factor = jnp.exp(tops - top[None, :])
    total = jnp.sum(every[:, 1] * factor, axis=0)
    weighted = jnp.sum(every[:, 2] * factor, axis=0)
    picked = jnp.sum(every[:, 3], axis=0)
    lse = top + jnp.log(total)
    logprob = picked - lse
    entropy = lse - weighted / total
    return (jnp.where(own_live, logprob, 0.0), jnp.where(own_live, entropy, 0.0))


def solution(mesh):
    ny, nz = dp_grid(mesh)
    return jax.shard_map(
        functools.partial(local, ny, nz),
        mesh=mesh,
        in_specs=(P("dp", "vocab"), P(), P("dp", "vocab"), P("dp"), P(), P()),
        out_specs=(P("dp"), P("dp")),
        check_vma=False,
    )
```

time: 172 us -> 178 us (1.035)
  Pallas kernels: 122 us -> 128 us
    pallas_call x1, Pallas kernels: 107 us -> 113 us  [gather_head(): pl.pallas_call(functools.partial(head_gather_kernel, ny, nz, split), out_...]
  transfers between devices with their start and end apart: 1 -> 1, of which waited for: 0 -> 0; matrix products, arithmetic and copies ran while one was open for 0% -> 0% of each run, Pallas kernels for 62% -> 64%
where the time goes in v3:
time: 178 us; the launch traced here: 177 us
  Pallas kernels  128 us (72%)
  matrix products  20.9 us (12%)
  between operations  14.2 us (8%)
  other arithmetic  12.8 us (7%)
    pallas_call x1, Pallas kernels, gather_head(): pl.pallas_call(functools.partial(head_gather_kernel, ny, nz, split), out_...  113 us
    dot_general x1, matrix products, local(): logits = jnp.dot(normed, columns, preferred_element_type=jnp.float32)  20.9 us
    pallas_call x1, Pallas kernels, exchange_stats(): pl.pallas_call(functools.partial(stats_kernel, n), out_shape=jax.ShapeDty...  15.1 us
    reduce_sum x1, other arithmetic, local(): total_local = jnp.sum(expo, axis=1)  6.98 us
  transfers between devices with their start and end apart: 1, of which 0 were waited for; matrix products, arithmetic and copies ran while one was open for 0% of the time, Pallas kernels for 64%

profile of v3, /device:TPU:1, one launch (start us, length us, event | category | flops | bytes accessed | tf_op | source)
XLA Modules:
  0.0 177.4 jit_solution(14308480691945082381)
XLA Ops:
  7.2 0.0 copy-start
  7.2 0.0 copy-start.2
  7.2 0.0 copy-start.3
  7.2 0.0 copy-start.1
  7.2 0.0 all-gather.2.cloned.1.call-start
  7.3 0.7 all-gather.2.cloned.1.call-update
  7.9 113.0 %shard_map.77 = bf16[4,8,64,4000]{3,2,1,0:T(8,128)(2,1)} custom-call(bf16[64,4000]{1,0:T(8,128)(2,1)} %head_ref.1), custom_call_target="tpu_custom_call" | custom-call | bytes 32768000 | tf_op jit(solution)/shard_map/pallas_call | solution.py:162
  121.0 0.0 copy-done
  121.0 0.0 copy-done.2
  121.0 0.0 copy-done.3
  121.0 0.1 select_reduce_fusion.1
  121.1 0.6 dynamic_slice.3
  121.8 0.0 copy-done.1
  121.8 0.0 all-gather.2.cloned.1.call-done
  121.8 2.6 %fusion.1 = f32[768]{0:T(1024)S(1)} fusion(bf16[768,2048]{1,0:T(8,128)(2,1)} %all-gather.2.cloned.1.call-done), kind=kLoop, calls=%fused_computation.7 | loop fusion | flops 4717824 | bytes 3148800 | tf_op jit(solution)/shard_map/reduce_sum | solution.py:235
  124.4 20.9 %fusion.14 = (f32[768]{0:T(1024)S(1)}, f32[768,4000]{0,1:T(8,128)}) fusion(bf16[2048,4000]{1,0:T(8,128)(2,1)} %bitcast.23, bf16[768,2048]{1,0:T(8,128)(2,1)} %all-gather.2.cloned.1.call-done, f32[2048]{0:T(1024)S(1)} %convert_element_type.10, f32[768]{0:T(1024)S(1)} %add_rsqrt_fusion), kind=kOutput, calls=%fused_computation.33 | convolution fusion | flops 12592274432 | bytes 31832064 | tf_op jit(solution)/shard_map/dot_general | solution.py:238
  145.3 7.0 %fusion = (f32[768]{0:T(1024)S(1)}, f32[768]{0:T(1024)S(1)}, f32[768]{0:T(1024)S(1)}) fusion(f32[768,4000]{0,1:T(8,128)} %get-tuple-element.17, f32[768]{0:T(1024)S(1)} %get-tuple-element.16, s32[768]{0:T(1024)S(1)} %broadcast_subtract_fusion), kind=kLoop, calls=%fused_computation.4 | loop fusion | flops 21501696 | bytes 12303360 | tf_op jit(solution)/shard_map/reduce_sum | solution.py:241
  152.3 0.6 pad_maximum_fusion.stats_ref
  152.9 15.1 %shard_map.78 = f32[8,4,768]{2,1,0:T(4,128)} custom-call(f32[4,768]{1,0:T(4,128)} %pad_maximum_fusion.stats_ref), custom_call_target="tpu_custom_call" | custom-call | tf_op jit(solution)/shard_map/pallas_call | solution.py:207
  168.1 1.2 fusion.13
  169.3 1.2 subtract_select_fusion
  (8 shorter events, 0.1 us)
Async XLA Ops:
  7.2 113.8 %copy-start = (bf16[2048]{0:T(1024)(128)(2,1)S(1)}, bf16[2048]{0:T(1024)(128)(2,1)}, u32[]{:S(2)}) copy-start(bf16[2048]{0:T(1024)(128)(2,1)} %param.7) | copy-start | bytes 12292
  7.2 113.8 %copy-start.2 = (s32[64]{0:T(128)S(1)}, s32[64]{0:T(128)}, u32[]{:S(2)}) copy-start(s32[64]{0:T(128)} %param.10) | copy-start | bytes 772
  7.2 113.8 %copy-start.3 = (s32[64]{0:T(128)S(1)}, s32[64]{0:T(128)}, u32[]{:S(2)}) copy-start(s32[64]{0:T(128)} %param.11) | copy-start | bytes 772
  7.2 114.6 %copy-start.1 = (s32[768]{0:T(1024)S(1)}, s32[768]{0:T(1024)}, u32[]{:S(2)}) copy-start(s32[768]{0:T(1024)} %param.9) | copy-start | bytes 9220
  7.2 114.6 %all-gather.2.cloned.1.call-start = ((), (), s32[]{:S(2)}) async-start(), calls=%async_computation | async-start | bytes 3538944 | tf_op jit(solution)/shard_map/all_gather | solution.py:231
Sparse Core Ops, SparseCore 0:
  9.9 38.3 all-gather.1

commit v4 on v2

--- a/solution.py
+++ b/solution.py
@@ -21,7 +21,8 @@
     return size // nz, nz
 
 
-def head_gather_kernel(ny, nz, head_ref, out_ref, send_sem, recv_sem, local_sem):
+def head_gather_kernel(ny, nz, nv, head_ref, hidden_ref, out_ref, feat_ref, send_sem, recv_sem,
+                       local_sem, hsend_sem, hrecv_sem, hlocal_sem):
     dp = lax.axis_index("dp")
     v = lax.axis_index("vocab")
     y = dp // nz
@@ -43,6 +44,7 @@
 
     barrier = pltpu.get_barrier_semaphore()
     peers = [dev(yr, z), dev(yl, z), dev(y, zs(1)), dev(y, zs(-1))]
+    peers += [(dp, (v + k) % nv) for k in range(1, nv)]
     for peer in peers:
         pl.semaphore_signal(barrier, inc=1, device_id=peer, device_id_type=MESH)
     pl.semaphore_wait(barrier, len(peers))
@@ -66,6 +68,23 @@
 
     local = pltpu.make_async_copy(head_ref, out_ref.at[y, z], local_sem)
     local.start()
+
+    breadth = hidden_ref.shape[1]
+    own_cols = feat_ref.at[:, pl.ds(pl.multiple_of(v * breadth, breadth), breadth)]
+    hidden_copies = []
+    for k in range(1, nv):
+        c = pltpu.make_async_remote_copy(
+            src_ref=hidden_ref,
+            dst_ref=own_cols,
+            send_sem=hsend_sem.at[k - 1],
+            recv_sem=hrecv_sem.at[k - 1],
+            device_id=(dp, (v + k) % nv),
+            device_id_type=MESH,
+        )
+        c.start()
+        hidden_copies.append(c)
+    hidden_local = pltpu.make_async_copy(hidden_ref, own_cols, hlocal_sem)
+    hidden_local.start()
 
     send("ay_r1", head_ref.at[0], out_ref.at[y, z, 0], dev(yr, z))
     send("ay_l1", head_ref.at[0], out_ref.at[y, z, 0], dev(yl, z))
@@ -159,30 +178,40 @@
     arrived(f"az_l{zsteps}")
     arrived(f"by_r{ysteps}")
     arrived(f"by_l{ysteps}")
-    for c in copies.values():
+    hidden_local.wait()
+    for c in hidden_copies:
+        c.wait_recv()
+    for c in list(copies.values()) + hidden_copies:
         c.wait_send()
 
 
-def gather_head(head, ny, nz):
+def gather_all(head, hidden, ny, nz, nv):
     rows, width = head.shape
+    slots, breadth = hidden.shape
     blocks = head.reshape(2, rows // 2, width)
     streams = 4 * (ny // 2 + nz // 2)
-    out = pl.pallas_call(
-        functools.partial(head_gather_kernel, ny, nz),
-        out_shape=jax.ShapeDtypeStruct((ny, nz, 2, rows // 2, width), head.dtype),
-        in_specs=[pl.BlockSpec(memory_space=pl.ANY)],
-        out_specs=pl.BlockSpec(memory_space=pl.ANY),
+    out, feat = pl.pallas_call(
+        functools.partial(head_gather_kernel, ny, nz, nv),
+        out_shape=(
+            jax.ShapeDtypeStruct((ny, nz, 2, rows // 2, width), head.dtype),
+            jax.ShapeDtypeStruct((slots, nv * breadth), hidden.dtype),
+        ),
+        in_specs=[pl.BlockSpec(memory_space=pl.ANY)] * 2,
+        out_specs=(pl.BlockSpec(memory_space=pl.ANY),) * 2,
         scratch_shapes=[
             pltpu.SemaphoreType.DMA((streams,)),
             pltpu.SemaphoreType.DMA((streams,)),
+            pltpu.SemaphoreType.DMA(()),
+            pltpu.SemaphoreType.DMA((nv - 1,)),
+            pltpu.SemaphoreType.DMA((nv - 1,)),
             pltpu.SemaphoreType.DMA(()),
         ],
         compiler_params=pltpu.CompilerParams(collective_id=0, has_side_effects=True),
         cost_estimate=pl.CostEstimate(
             flops=0, transcendentals=0, bytes_accessed=2 * ny * nz * rows * width * 2
         ),
-    )(blocks)
-    return out.reshape(ny * nz * rows, width)
+    )(blocks, hidden)
+    return out.reshape(ny * nz * rows, width), feat
 
 
 def stats_kernel(n, stats_ref, out_ref, send_sem, recv_sem):
@@ -235,8 +264,7 @@
     owners = jnp.arange(groups, dtype=jnp.int32)
     loads = jnp.sum(jnp.where(seq_owner[:, None] == owners[None, :], seq_lens[:, None], 0), axis=0)
     own_live = jnp.arange(slots, dtype=jnp.int32) < loads[position]
-    columns = gather_head(head, ny, nz)
-    features = lax.all_gather(hidden, "vocab", axis=1, tiled=True)
+    columns, features = gather_all(head, hidden, ny, nz, slices)
     wide = features.astype(jnp.float32)
     normed = (
         wide

time: 172 us -> 162 us (0.942)
  between operations: 14.2 us -> 0.73 us
  Pallas kernels: 122 us -> 126 us
    pallas_call x1, Pallas kernels: 107 us -> 112 us  [gather_all(): pl.pallas_call(functools.partial(head_gather_kernel, ny, nz, nv), out_sha...]
  transfers between devices with their start and end apart: 1 -> 0, of which waited for: 0 -> 0; matrix products, arithmetic and copies ran while one was open for 0% -> 0% of each run, Pallas kernels for 62% -> 0%
where the time goes in v4:
time: 162 us
  Pallas kernels  126 us (78%)
  matrix products  20.9 us (13%)
  other arithmetic  13.5 us (8%)
    pallas_call x1, Pallas kernels, gather_all(): pl.pallas_call(functools.partial(head_gather_kernel, ny, nz, nv), out_sha...  112 us
    dot_general x1, matrix products, local(): logits = jnp.dot(normed, columns, preferred_element_type=jnp.float32)  20.9 us
    pallas_call x1, Pallas kernels, exchange_stats(): pl.pallas_call(functools.partial(stats_kernel, n), out_shape=jax.ShapeDty...  14.5 us
    reduce_sum x1, other arithmetic, local(): total_local = jnp.sum(expo, axis=1)  6.99 us

profile of v4, /device:TPU:1, one launch (start us, length us, event | category | flops | bytes accessed | tf_op | source)
XLA Modules:
  0.0 162.2 jit_solution(17866375740415975618)
XLA Ops:
  0.6 111.9 %shard_map.77 = (bf16[4,8,2,32,4000]{4,3,2,1,0:T(8,128)(2,1)}, bf16[768,2048]{1,0:T(8,128)(2,1)}) custom-call(bf16[2,32,4000]{2,1,0:T(8,128)(2,1)} %bitcast.24, bf16[768,256]{1,0:T(8,128)(2,1)} %hidden_ref.1), custom_call_target="tpu_custom_call" | custom-call | bytes 32768000 | tf_op jit(solution)/shard_map/pallas_call | solution.py:193
  112.5 2.6 %fusion.1 = f32[768]{0:T(1024)S(1)} fusion(bf16[768,2048]{1,0:T(8,128)(2,1)} %get-tuple-element.4), kind=kLoop, calls=%fused_computation.7 | loop fusion | flops 4717824 | bytes 3148800 | tf_op jit(solution)/shard_map/reduce_sum | solution.py:271
  115.1 0.7 convert_element_type.10
  115.8 0.0 copy-start
  115.8 20.9 %fusion.14 = (f32[768]{0:T(1024)S(1)}, f32[768,4000]{0,1:T(8,128)}) fusion(bf16[2048,4000]{1,0:T(8,128)(2,1)} %bitcast.25, bf16[768,2048]{1,0:T(8,128)(2,1)} %get-tuple-element.4, f32[2048]{0:T(1024)S(1)} %convert_element_type.10, f32[768]{0:T(1024)S(1)} %add_rsqrt_fusion), kind=kOutput, calls=%fused_computation.33 | convolution fusion | flops 12592274432 | bytes 31832064 | tf_op jit(solution)/shard_map/dot_general | solution.py:274
  136.7 0.0 copy-start.1
  136.7 0.0 copy-start.2
  136.7 0.0 copy-done
  136.7 7.0 %fusion = (f32[768]{0:T(1024)S(1)}, f32[768]{0:T(1024)S(1)}, f32[768]{0:T(1024)S(1)}) fusion(f32[768,4000]{0,1:T(8,128)} %get-tuple-element.21, f32[768]{0:T(1024)S(1)} %get-tuple-element.20, s32[768]{0:T(1024)S(1)} %broadcast_subtract_fusion), kind=kLoop, calls=%fused_computation.4 | loop fusion | flops 21501696 | bytes 12303360 | tf_op jit(solution)/shard_map/reduce_sum | solution.py:277
  143.8 0.6 pad_maximum_fusion.stats_ref
  144.4 14.5 %shard_map.78 = f32[8,4,768]{2,1,0:T(4,128)} custom-call(f32[4,768]{1,0:T(4,128)} %pad_maximum_fusion.stats_ref), custom_call_target="tpu_custom_call" | custom-call | tf_op jit(solution)/shard_map/pallas_call | solution.py:244
  158.9 1.2 fusion.13
  160.1 0.0 copy-done.1
  160.1 0.0 copy-done.2
  160.1 0.1 select_reduce_fusion.1
  160.2 0.7 dynamic_slice.3
  160.9 1.3 subtract_select_fusion
  (7 shorter events, 0.1 us)
Async XLA Ops:
  115.8 20.9 %copy-start = (s32[768]{0:T(1024)S(1)}, s32[768]{0:T(1024)}, u32[]{:S(2)}) copy-start(s32[768]{0:T(1024)} %param.9) | copy-start | bytes 9220
  136.7 23.4 %copy-start.1 = (s32[64]{0:T(128)S(1)}, s32[64]{0:T(128)}, u32[]{:S(2)}) copy-start(s32[64]{0:T(128)} %param.10) | copy-start | bytes 772
  136.7 23.4 %copy-start.2 = (s32[64]{0:T(128)S(1)}, s32[64]{0:T(128)}, u32[]{:S(2)}) copy-start(s32[64]{0:T(128)} %param.11) | copy-start | bytes 772

commit v5 on v4

--- a/solution.py
+++ b/solution.py
@@ -196,7 +196,7 @@
             jax.ShapeDtypeStruct((ny, nz, 2, rows // 2, width), head.dtype),
             jax.ShapeDtypeStruct((slots, nv * breadth), hidden.dtype),
         ),
-        in_specs=[pl.BlockSpec(memory_space=pl.ANY)] * 2,
+        in_specs=[pl.BlockSpec(memory_space=pltpu.VMEM)] * 2,
         out_specs=(pl.BlockSpec(memory_space=pl.ANY),) * 2,
         scratch_shapes=[
             pltpu.SemaphoreType.DMA((streams,)),

time: 162 us -> 163 us (level)
  no operation moved by 1% of the time
where the time goes in v5:
time: 163 us
  Pallas kernels  127 us (78%)
  matrix products  20.9 us (13%)
  other arithmetic  13.5 us (8%)
    pallas_call x1, Pallas kernels, gather_all(): pl.pallas_call(functools.partial(head_gather_kernel, ny, nz, nv), out_sha...  113 us
    dot_general x1, matrix products, local(): logits = jnp.dot(normed, columns, preferred_element_type=jnp.float32)  20.9 us
    pallas_call x1, Pallas kernels, exchange_stats(): pl.pallas_call(functools.partial(stats_kernel, n), out_shape=jax.ShapeDty...  14.5 us
    reduce_sum x1, other arithmetic, local(): total_local = jnp.sum(expo, axis=1)  6.99 us

profile of v5, /device:TPU:1, one launch (start us, length us, event | category | flops | bytes accessed | tf_op | source)
XLA Modules:
  0.0 163.1 jit_solution(5536633391882626544)
XLA Ops:
  0.6 112.7 %shard_map.77 = (bf16[4,8,2,32,4000]{4,3,2,1,0:T(8,128)(2,1)}, bf16[768,2048]{1,0:T(8,128)(2,1)}) custom-call(bf16[2,32,4000]{2,1,0:T(8,128)(2,1)} %bitcast.24, bf16[768,256]{1,0:T(8,128)(2,1)} %hidden_ref.1), custom_call_target="tpu_custom_call" | custom-call | bytes 32768000 | tf_op jit(solution)/shard_map/pallas_call | solution.py:193
  113.4 2.6 %fusion.1 = f32[768]{0:T(1024)S(1)} fusion(bf16[768,2048]{1,0:T(8,128)(2,1)} %get-tuple-element.4), kind=kLoop, calls=%fused_computation.7 | loop fusion | flops 4717824 | bytes 3148800 | tf_op jit(solution)/shard_map/reduce_sum | solution.py:271
  116.0 0.7 convert_element_type.10
  116.7 0.0 copy-start
  116.7 20.9 %fusion.14 = (f32[768]{0:T(1024)S(1)}, f32[768,4000]{0,1:T(8,128)}) fusion(bf16[2048,4000]{1,0:T(8,128)(2,1)} %bitcast.25, bf16[768,2048]{1,0:T(8,128)(2,1)} %get-tuple-element.4, f32[2048]{0:T(1024)S(1)} %convert_element_type.10, f32[768]{0:T(1024)S(1)} %add_rsqrt_fusion), kind=kOutput, calls=%fused_computation.33 | convolution fusion | flops 12592274432 | bytes 31832064 | tf_op jit(solution)/shard_map/dot_general | solution.py:274
  137.6 0.0 copy-start.1
  137.6 0.0 copy-start.2
  137.6 0.0 copy-done
  137.6 7.0 %fusion = (f32[768]{0:T(1024)S(1)}, f32[768]{0:T(1024)S(1)}, f32[768]{0:T(1024)S(1)}) fusion(f32[768,4000]{0,1:T(8,128)} %get-tuple-element.21, f32[768]{0:T(1024)S(1)} %get-tuple-element.20, s32[768]{0:T(1024)S(1)} %broadcast_subtract_fusion), kind=kLoop, calls=%fused_computation.4 | loop fusion | flops 21501696 | bytes 12303360 | tf_op jit(solution)/shard_map/reduce_sum | solution.py:277
  144.6 0.6 pad_maximum_fusion.stats_ref
  145.3 14.5 %shard_map.78 = f32[8,4,768]{2,1,0:T(4,128)} custom-call(f32[4,768]{1,0:T(4,128)} %pad_maximum_fusion.stats_ref), custom_call_target="tpu_custom_call" | custom-call | tf_op jit(solution)/shard_map/pallas_call | solution.py:244
  159.7 1.2 fusion.13
  161.0 0.0 copy-done.1
  161.0 0.0 copy-done.2
  161.0 0.1 select_reduce_fusion.1
  161.1 0.7 dynamic_slice.3
  161.8 1.3 subtract_select_fusion
  (7 shorter events, 0.1 us)
Async XLA Ops:
  116.7 20.9 %copy-start = (s32[768]{0:T(1024)S(1)}, s32[768]{0:T(1024)}, u32[]{:S(2)}) copy-start(s32[768]{0:T(1024)} %param.9) | copy-start | bytes 9220
  137.6 23.4 %copy-start.1 = (s32[64]{0:T(128)S(1)}, s32[64]{0:T(128)}, u32[]{:S(2)}) copy-start(s32[64]{0:T(128)} %param.10) | copy-start | bytes 772
  137.6 23.4 %copy-start.2 = (s32[64]{0:T(128)S(1)}, s32[64]{0:T(128)}, u32[]{:S(2)}) copy-start(s32[64]{0:T(128)} %param.11) | copy-start | bytes 772

commit v6 on v5

v6 whole, which is shorter than its diff:
```python
import functools

import jax
import jax.numpy as jnp
from jax import lax
from jax.experimental import pallas as pl
from jax.experimental.pallas import tpu as pltpu
from jax.sharding import PartitionSpec as P

EPS = 1e-05
MESH = pl.DeviceIdType.MESH


def dp_grid(mesh):
    size = mesh.shape["dp"]
    try:
        zs = {tuple(mesh.devices[i, 0].coords)[2] for i in range(size)}
        nz = len(zs)
    except Exception:
        nz = size // 4
    return size // nz, nz


class Ring:
    def __init__(self, ny, nz, send_sem, recv_sem):
        self.ny, self.nz = ny, nz
        self.dp = lax.axis_index("dp")
        self.v = lax.axis_index("vocab")
        self.y = self.dp // nz
        self.z = self.dp % nz
        self.send_sem, self.recv_sem = send_sem, recv_sem
        self.copies = {}
        self.right_y, self.left_y = self.dev(self.ys(1), self.z), self.dev(self.ys(-1), self.z)
        self.right_z, self.left_z = self.dev(self.y, self.zs(1)), self.dev(self.y, self.zs(-1))

    def zs(self, k):
        return (self.z + k + 8 * self.nz) % self.nz

    def ys(self, k):
        return (self.y + k + 8 * self.ny) % self.ny

    def dev(self, yy, zz):
        return (yy * self.nz + zz, self.v)

    def send(self, key, view, peer, src=None):
        c = pltpu.make_async_remote_copy(
            src_ref=view if src is None else src,
            dst_ref=view,
            send_sem=self.send_sem.at[len(self.copies)],
            recv_sem=self.recv_sem.at[len(self.copies)],
            device_id=peer,
            device_id_type=MESH,
        )
        self.copies[key] = c
        c.start()

    def arrived(self, key):
        self.copies[key].wait_recv()

    def drain(self):
        for c in self.copies.values():
            c.wait_send()


def phase_one_kernel(ny, nz, nv, head_ref, hidden_ref, out_ref, feat_ref, send_sem, recv_sem,
                     local_sem, hsend_sem, hrecv_sem, hlocal_sem):
    ring = Ring(ny, nz, send_sem, recv_sem)
    y, z, v, dp = ring.y, ring.z, ring.v, ring.dp
    rows = head_ref.shape[1]
    hr = rows // 2

    barrier = pltpu.get_barrier_semaphore()
    peers = [ring.right_y, ring.left_y, ring.right_z, ring.left_z]
    peers += [(dp, (v + k) % nv) for k in range(1, nv)]
    for peer in peers:
        pl.semaphore_signal(barrier, inc=1, device_id=peer, device_id_type=MESH)
    pl.semaphore_wait(barrier, len(peers))

    local = pltpu.make_async_copy(head_ref, out_ref.at[y, z], local_sem)
    local.start()
    breadth = hidden_ref.shape[1]
    own_cols = feat_ref.at[:, pl.ds(pl.multiple_of(v * breadth, breadth), breadth)]
    hidden_copies = []
    for k in range(1, nv):
        c = pltpu.make_async_remote_copy(
            src_ref=hidden_ref,
            dst_ref=own_cols,
            send_sem=hsend_sem.at[k - 1],
            recv_sem=hrecv_sem.at[k - 1],
            device_id=(dp, (v + k) % nv),
            device_id_type=MESH,
        )
        c.start()
        hidden_copies.append(c)
    hidden_local = pltpu.make_async_copy(hidden_ref, own_cols, hlocal_sem)
    hidden_local.start()

    def single_y(step):
        if step == 1:
            ring.send("ay1", out_ref.at[y, z, 0], ring.right_y, head_ref.at[0])
            ring.send("ay1l", out_ref.at[y, z, 0], ring.left_y, head_ref.at[0])
            return
        src_r, src_l = ring.ys(-(step - 1)), ring.ys(step - 1)
        if step < ny - step:
            ring.send(f"ay{step}", out_ref.at[src_r, z, 0], ring.right_y)
            ring.send(f"ay{step}l", out_ref.at[src_l, z, 0], ring.left_y)
        else:
            ring.send(f"ay{step}", out_ref.at[src_r, z, 0, pl.ds(0, hr)], ring.right_y)
            ring.send(f"ay{step}l", out_ref.at[src_l, z, 0, pl.ds(hr, rows - hr)], ring.left_y)

    def single_z(step):
        if step == 1:
            ring.send("bz1", out_ref.at[y, z, 1], ring.right_z, head_ref.at[1])
            ring.send("bz1l", out_ref.at[y, z, 1], ring.left_z, head_ref.at[1])
            return
        src_r, src_l = ring.zs(-(step - 1)), ring.zs(step - 1)
        if step < nz - step:
            ring.send(f"bz{step}", out_ref.at[y, src_r, 1], ring.right_z)
            ring.send(f"bz{step}l", out_ref.at[y, src_l, 1], ring.left_z)
        else:
            ring.send(f"bz{step}", out_ref.at[y, src_r, 1, pl.ds(0, hr)], ring.right_z)
            ring.send(f"bz{step}l", out_ref.at[y, src_l, 1, pl.ds(hr, rows - hr)], ring.left_z)

    ysteps, zsteps = ny // 2, nz // 2
    single_y(1)
    single_z(1)
    for step in range(2, max(ysteps, zsteps) + 1):
        if step <= ysteps:
            ring.arrived(f"ay{step - 1}")
            ring.arrived(f"ay{step - 1}l")
            single_y(step)
        if step <= zsteps:
            ring.arrived(f"bz{step - 1}")
            ring.arrived(f"bz{step - 1}l")
            single_z(step)
    ring.arrived(f"ay{ysteps}")
    ring.arrived(f"ay{ysteps}l")
    ring.arrived(f"bz{zsteps}")
    ring.arrived(f"bz{zsteps}l")
    local.wait()
    hidden_local.wait()
    for c in hidden_copies:
        c.wait_recv()
    ring.drain()
    for c in hidden_copies:
        c.wait_send()


def phase_two_kernel(ny, nz, h_in, np0_ref, np1_ref, ids_ref, out_ref,
                     top_ref, total_ref, weighted_ref, picked_ref,
                     send_sem, recv_sem, stage_a, stage_b, stage_sem, acc):
    del h_in
    ring = Ring(ny, nz, send_sem, recv_sem)
    y, z = ring.y, ring.z
    rows, width = out_ref.shape[3], out_ref.shape[4]
    ka, kb = ny * rows, nz * rows

    barrier = pltpu.get_barrier_semaphore()
    peers = [ring.right_y, ring.left_y, ring.right_z, ring.left_z]
    for peer in peers:
        pl.semaphore_signal(barrier, inc=1, device_id=peer, device_id_type=MESH)
    pl.semaphore_wait(barrier, len(peers))

    state = {"first": True}

    def accumulate(lhs, rhs):
        part = jnp.dot(lhs, rhs, preferred_element_type=jnp.float32)
        if state["first"]:
            acc[...] = part
            state["first"] = False
        else:
            acc[...] += part

    def use_a(zz):
        c = pltpu.make_async_copy(out_ref.at[:, zz, 0], stage_a, stage_sem.at[0])
        c.start()
        c.wait()
        lhs = np0_ref[:, pl.ds(pl.multiple_of(zz * ka, ka), ka)]
        accumulate(lhs, stage_a[...].reshape(ka, width))

    def use_b(yy):
        c = pltpu.make_async_copy(out_ref.at[yy, :, 1], stage_b, stage_sem.at[1])
        c.start()
        c.wait()
        lhs = np1_ref[:, pl.ds(pl.multiple_of(yy * kb, kb), kb)]
        accumulate(lhs, stage_b[...].reshape(kb, width))

    def group_z(step):
        src_r, src_l = ring.zs(-(step - 1)), ring.zs(step - 1)
        if step < nz - step:
            ring.send(f"az{step}", out_ref.at[:, src_r, 0], ring.right_z)
            ring.send(f"az{step}l", out_ref.at[:, src_l, 0], ring.left_z)
        else:
            half = ny // 2
            ring.send(f"az{step}", out_ref.at[pl.ds(0, half), src_r, 0], ring.right_z)
            ring.send(f"az{step}l", out_ref.at[pl.ds(half, ny - half), src_l, 0], ring.left_z)

    def group_y(step):
        src_r, src_l = ring.ys(-(step - 1)), ring.ys(step - 1)
        if step < ny - step:
            ring.send(f"by{step}", out_ref.at[src_r, :, 1], ring.right_y)
            ring.send(f"by{step}l", out_ref.at[src_l, :, 1], ring.left_y)
        else:
            half = nz // 2
            ring.send(f"by{step}", out_ref.at[src_r, pl.ds(0, half), 1], ring.right_y)
            ring.send(f"by{step}l", out_ref.at[src_l, pl.ds(half, nz - half), 1], ring.left_y)

    ysteps, zsteps = ny // 2, nz // 2
    group_z(1)
    group_y(1)
    use_a(z)
    use_b(y)
    for step in range(2, max(ysteps, zsteps) + 1):
        if step <= zsteps:
            ring.arrived(f"az{step - 1}")
            ring.arrived(f"az{step - 1}l")
            group_z(step)
        if step <= ysteps:
            ring.arrived(f"by{step - 1}")
            ring.arrived(f"by{step - 1}l")
            group_y(step)
        if step <= zsteps:
            use_a(ring.zs(-(step - 1)))
            use_a(ring.zs(step - 1))
        if step <= ysteps:
            use_b(ring.ys(-(step - 1)))
            use_b(ring.ys(step - 1))
    ring.arrived(f"az{zsteps}")
    ring.arrived(f"az{zsteps}l")
    use_a(ring.zs(zsteps))
    ring.arrived(f"by{ysteps}")
    ring.arrived(f"by{ysteps}l")
    use_b(ring.ys(ysteps))

    tile = 32
    slots = acc.shape[0]

    def stats(i, carry):
        r = pl.ds(pl.multiple_of(i * tile, tile), tile)
        logits = acc[r, :]
        top = jnp.max(logits, axis=1, keepdims=True)
        expo = jnp.exp(logits - top)
        total = jnp.sum(expo, axis=1, keepdims=True)
        weighted = jnp.sum(expo * logits, axis=1, keepdims=True)
        ids = lax.broadcasted_iota(jnp.int32, logits.shape, 1)
        picked = jnp.sum(jnp.where(ids == ids_ref[r, :], logits, 0.0), axis=1, keepdims=True)
        top_ref[r, :] = top
        total_ref[r, :] = total
        weighted_ref[r, :] = weighted
        picked_ref[r, :] = picked
        return carry

    lax.fori_loop(0, slots // tile, stats, 0)
    ring.drain()


def gather_phase_one(head, hidden, ny, nz, nv):
    rows, width = head.shape
    slots, breadth = hidden.shape
    blocks = head.reshape(2, rows // 2, width)
    streams = 2 * (ny // 2 + nz // 2)
    return pl.pallas_call(
        functools.partial(phase_one_kernel, ny, nz, nv),
        out_shape=(
            jax.ShapeDtypeStruct((ny, nz, 2, rows // 2, width), head.dtype),
            jax.ShapeDtypeStruct((slots, nv * breadth), hidden.dtype),
        ),
        in_specs=[pl.BlockSpec(memory_space=pltpu.VMEM)] * 2,
        out_specs=(pl.BlockSpec(memory_space=pl.ANY),) * 2,
        scratch_shapes=[
            pltpu.SemaphoreType.DMA((streams,)),
            pltpu.SemaphoreType.DMA((streams,)),
            pltpu.SemaphoreType.DMA(()),
            pltpu.SemaphoreType.DMA((nv - 1,)),
            pltpu.SemaphoreType.DMA((nv - 1,)),
            pltpu.SemaphoreType.DMA(()),
        ],
        compiler_params=pltpu.CompilerParams(collective_id=0, has_side_effects=True),
        cost_estimate=pl.CostEstimate(
            flops=0, transcendentals=0, bytes_accessed=4 * (ny + nz) * rows * width
        ),
    )(blocks, hidden)


def gather_phase_two(h, np0, np1, ids, ny, nz):
    _, _, _, rows, width = h.shape
    slots = np0.shape[0]
    streams = 2 * (ny // 2 + nz // 2)
    col = jax.ShapeDtypeStruct((slots, 1), jnp.float32)
    vmem = pl.BlockSpec(memory_space=pltpu.VMEM)
    outs = pl.pallas_call(
        functools.partial(phase_two_kernel, ny, nz),
        out_shape=(jax.ShapeDtypeStruct(h.shape, h.dtype), col, col, col, col),
        in_specs=[pl.BlockSpec(memory_space=pl.ANY), vmem, vmem, vmem],
        out_specs=(pl.BlockSpec(memory_space=pl.ANY), vmem, vmem, vmem, vmem),
        scratch_shapes=[
            pltpu.SemaphoreType.DMA((streams,)),
            pltpu.SemaphoreType.DMA((streams,)),
            pltpu.VMEM((ny, rows, width), h.dtype),
            pltpu.VMEM((nz, rows, width), h.dtype),
            pltpu.SemaphoreType.DMA((2,)),
            pltpu.VMEM((slots, width), jnp.float32),
        ],
        input_output_aliases={0: 0},
        compiler_params=pltpu.CompilerParams(
            collective_id=2, has_side_effects=True, vmem_limit_bytes=60 * 1024 * 1024
        ),
        cost_estimate=pl.CostEstimate(
            flops=2 * slots * ny * nz * 2 * rows * width,
            transcendentals=slots * width,
            bytes_accessed=4 * ny * nz * rows * width,
        ),
    )(h, np0, np1, ids)
    return outs[1:]


def stats_kernel(n, stats_ref, out_ref, send_sem, recv_sem):
    dp = lax.axis_index("dp")
    v = lax.axis_index("vocab")
    barrier = pltpu.get_barrier_semaphore()
    for k in range(1, n):
        pl.semaphore_signal(barrier, inc=1, device_id=(dp, (v + k) % n), device_id_type=MESH)
    pl.semaphore_wait(barrier, n - 1)
    copies = []
    for k in range(1, n):
        c = pltpu.make_async_remote_copy(
            src_ref=stats_ref,
            dst_ref=out_ref.at[v],
            send_sem=send_sem.at[k - 1],
            recv_sem=recv_sem.at[k - 1],
            device_id=(dp, (v + k) % n),
            device_id_type=MESH,
        )
        c.start()
        copies.append(c)
    out_ref[v] = stats_ref[...]
    for c in copies:
        c.wait_recv()
    for c in copies:
        c.wait_send()


def exchange_stats(stats, n):
    return pl.pallas_call(
        functools.partial(stats_kernel, n),
        out_shape=jax.ShapeDtypeStruct((n,) + stats.shape, stats.dtype),
        in_specs=[pl.BlockSpec(memory_space=pltpu.VMEM)],
        out_specs=pl.BlockSpec(memory_space=pltpu.VMEM),
        scratch_shapes=[
            pltpu.SemaphoreType.DMA((n - 1,)),
            pltpu.SemaphoreType.DMA((n - 1,)),
        ],
        compiler_params=pltpu.CompilerParams(collective_id=1, has_side_effects=True),
    )(stats)


def local(ny, nz, hidden, gain, head, target_ids, seq_lens, seq_owner):
    groups = lax.axis_size("dp")
    slices = lax.axis_size("vocab")
    position = lax.axis_index("dp")
    slice_index = lax.axis_index("vocab")
    slots = hidden.shape[0]
    rows, breadth = head.shape
    owners = jnp.arange(groups, dtype=jnp.int32)
    loads = jnp.sum(jnp.where(seq_owner[:, None] == owners[None, :], seq_lens[:, None], 0), axis=0)
    own_live = jnp.arange(slots, dtype=jnp.int32) < loads[position]
    h, features = gather_phase_one(head, hidden, ny, nz, slices)
    wide = features.astype(jnp.float32)
    normed = (
        wide
        * lax.rsqrt(jnp.mean(wide * wide, axis=1, keepdims=True) + EPS)
        * gain.astype(jnp.float32)
    ).astype(jnp.bfloat16)
    split = normed.reshape(slots, ny, nz, 2, rows // 2)
    np0 = split[:, :, :, 0, :].transpose(0, 2, 1, 3).reshape(slots, nz * ny * (rows // 2))
    np1 = split[:, :, :, 1, :].reshape(slots, ny * nz * (rows // 2))
    local_id = (target_ids - slice_index * breadth).reshape(slots, 1)
    top_c, total_c, weighted_c, picked_c = gather_phase_two(h, np0, np1, local_id, ny, nz)
    stats = jnp.stack([top_c[:, 0], total_c[:, 0], weighted_c[:, 0], picked_c[:, 0]])
    every = exchange_stats(stats, slices)
    tops = every[:, 0]
    top = jnp.max(tops, axis=0)
    factor = jnp.exp(tops - top[None, :])
    total = jnp.sum(every[:, 1] * factor, axis=0)
    weighted = jnp.sum(every[:, 2] * factor, axis=0)
    picked = jnp.sum(every[:, 3], axis=0)
    lse = top + jnp.log(total)
    logprob = picked - lse
    entropy = lse - weighted / total
    return (jnp.where(own_live, logprob, 0.0), jnp.where(own_live, entropy, 0.0))


def solution(mesh):
    ny, nz = dp_grid(mesh)
    return jax.shard_map(
        functools.partial(local, ny, nz),
        mesh=mesh,
        in_specs=(P("dp", "vocab"), P(), P("dp", "vocab"), P("dp"), P(), P()),
        out_specs=(P("dp"), P("dp")),
        check_vma=False,
    )
```

time: 163 us -> 198 us (1.21)
  Pallas kernels: 127 us -> 170 us
  matrix products: 20.9 us -> 0 us
  local copies, waits for them, and re-layouts: 0.7 us -> 11.3 us
    pallas_call x1 -> x2, Pallas kernels: 113 us -> 163 us  [the longest x1 117 us: gather_phase_two(): pl.pallas_call(functools.partial(phase_two_kernel, ny, nz), out_shape=(ja...]
    dot_general x1 -> x0, matrix products: 20.9 us -> none  [local(): logits = jnp.dot(normed, columns, preferred_element_type=jnp.float32)]
    pallas_call x1, Pallas kernels: 14.5 us -> 7.44 us  [exchange_stats(): pl.pallas_call(functools.partial(stats_kernel, n), out_shape=jax.ShapeDty...]
    reduce_sum x1 -> x0, other arithmetic: 6.99 us -> none  [local(): total_local = jnp.sum(expo, axis=1)]
    pallas_call x0 -> x4, other arithmetic: none -> 4.67 us  [gather_phase_two(): pl.pallas_call(functools.partial(phase_two_kernel, ny, nz), out_shape=(ja...]
    convert_element_type x0 -> x1, local copies, waits for them, and re-layouts: none -> 3.18 us  [local(): normed = (wide * lax.rsqrt(jnp.mean(wide * wide, axis=1, keepdims=True) +...]
    another operation x4 -> x5, local copies, waits for them, and re-layouts: 0.02 us -> 2.74 us  [the longest x1 2.72 us: local(): np1 = split[:, :, :, 1, :].reshape(slots, ny * nz * (rows // 2))]
    reshape x0 -> x2, local copies, waits for them, and re-layouts: none -> 2.57 us  [the longest x1 1.64 us: local(): split[:, :, :, 0, :].transpose(0, 2, 1, 3)]
where the time goes in v6:
time: 198 us; the launch traced here: 197 us
  Pallas kernels  170 us (86%)
  other arithmetic  15.1 us (8%)
  local copies, waits for them, and re-layouts  11.3 us (6%)
    pallas_call x1, Pallas kernels, gather_phase_two(): pl.pallas_call(functools.partial(phase_two_kernel, ny, nz), out_shape=(ja...  117 us
    pallas_call x1, Pallas kernels, gather_phase_one(): pl.pallas_call(functools.partial(phase_one_kernel, ny, nz, nv), out_shape...  45.5 us
    pallas_call x1, Pallas kernels, exchange_stats(): pl.pallas_call(functools.partial(stats_kernel, n), out_shape=jax.ShapeDty...  7.44 us
    pallas_call x4, other arithmetic, gather_phase_two(): pl.pallas_call(functools.partial(phase_two_kernel, ny, nz), out_shape=(ja...  4.67 us

profile of v6, /device:TPU:1, one launch (start us, length us, event | category | flops | bytes accessed | tf_op | source)
XLA Modules:
  0.0 197.3 jit_solution(14372730245241535565)
XLA Ops:
  0.6 0.8 select_reduce_fusion
  1.4 0.7 dynamic_slice.3
  2.1 0.7 broadcast_subtract_fusion
  2.8 0.7 convert_element_type.10
  3.5 0.9 reshape.32.ids_ref
  4.4 45.5 %shard_map.77 = (bf16[4,8,2,32,4000]{4,3,2,1,0:T(8,128)(2,1)}, bf16[768,2048]{1,0:T(8,128)(2,1)}) custom-call(bf16[2,32,4000]{2,1,0:T(8,128)(2,1)} %bitcast.32, bf16[768,256]{1,0:T(8,128)(2,1)} %hidden_ref.1), custom_call_target="tpu_custom_call" | custom-call | bytes 12288000 | tf_op jit(solution)/shard_map/pallas_call | solution.py:262
  49.9 0.0 copy-start
  49.9 2.7 %fusion = f32[768]{0:T(1024)S(1)} fusion(bf16[768,2048]{1,0:T(8,128)(2,1)} %get-tuple-element.9), kind=kLoop, calls=%fused_computation.2 | loop fusion | flops 4717824 | bytes 3148800 | tf_op jit(solution)/shard_map/reduce_sum | solution.py:371
  52.6 0.1 copy-done
  52.7 2.5 %fusion.2 = bf16[768,2048]{1,0:T(8,128)(2,1)} fusion(bf16[768,2048]{1,0:T(8,128)(2,1)S(1)} %copy-done, f32[2048]{0:T(1024)S(1)} %convert_element_type.10, f32[768]{0:T(1024)S(1)} %add_rsqrt_fusion), kind=kLoop, calls=%fused_computation.4 | loop fusion | flops 6291456 | bytes 6302720 | tf_op jit(solution)/shard_map/convert_element_type | solution.py:373
  55.1 3.2 %copy.20 = bf16[768,2048]{0,1:T(8,128)(2,1)S(1)} copy(bf16[768,2048]{1,0:T(8,128)(2,1)} %fusion.2) | data formatting | bytes 6291456 | tf_op jit(solution)/shard_map/convert_element_type | solution.py:373
  58.3 1.9 fusion.8
  60.2 0.0 copy-start.1
  60.2 2.7 %copy.23.np1_ref = bf16[768,1024]{1,0:T(8,128)(2,1)} copy(bf16[768,1024]{0,1:T(8,128)(2,1)} %bitcast.31) | data formatting | bytes 3145728 | tf_op jit(solution)/shard_map/reshape;squeeze | solution.py:376
  62.9 0.0 copy-done.1
  63.0 0.1 copy.21
  63.1 1.6 copy.22.np0_ref
  64.7 117.3 %shard_map.78 = (bf16[4,8,2,32,4000]{4,3,2,1,0:T(8,128)(2,1)}, f32[768,1]{1,0:T(8,128)}, f32[768,1]{1,0:T(8,128)}, f32[768,1]{1,0:T(8,128)}, f32[768,1]{1,0:T(8,128)}) custom-call(bf16[4,8,2,32,4000]{4,3,2,1,0:T(8,128)(2,1)} %get-tuple-element.8.h_in, bf16[768,1024]{1,0:T(8,128)(2,1)} %copy.22.np0_ref, ...), custom_call_target="tpu_custom_call", output_to_operand_aliasing={{0}: (0, {})} | custom-call | flops 12582912000 | bytes 16384000 | tf_op jit(solution)/shard_map/pallas_call | solution.py:291
  182.0 1.2 reduce.2
  183.2 1.2 reduce.3
  184.4 1.2 reduce.4
  185.6 1.2 reduce.5
  186.8 0.6 pad_maximum_fusion.stats_ref
  187.4 7.4 %shard_map.79 = f32[8,4,768]{2,1,0:T(4,128)} custom-call(f32[4,768]{1,0:T(4,128)} %pad_maximum_fusion.stats_ref), custom_call_target="tpu_custom_call" | custom-call | tf_op jit(solution)/shard_map/pallas_call | solution.py:344
  194.9 1.2 fusion.9
  196.1 1.2 subtract_select_fusion
  (6 shorter events, 0.1 us)
Async XLA Ops:
  49.9 2.8 %copy-start = (bf16[768,2048]{1,0:T(8,128)(2,1)S(1)}, bf16[768,2048]{1,0:T(8,128)(2,1)}, u32[]{:S(2)}) copy-start(bf16[768,2048]{1,0:T(8,128)(2,1)} %get-tuple-element.9) | copy-start | bytes 9437188
  60.2 2.7 %copy-start.1 = (bf16[768,8,4,32]{0,3,1,2:T(8,128)(2,1)S(1)}, bf16[768,8,4,32]{0,3,1,2:T(8,128)(2,1)}, u32[]{:S(2)}) copy-start(bf16[768,8,4,32]{0,3,1,2:T(8,128)(2,1)} %get-tuple-element.19) | copy-start | bytes 4718596

commit v7 on v4

--- a/solution.py
+++ b/solution.py
@@ -86,98 +86,78 @@
     hidden_local = pltpu.make_async_copy(hidden_ref, own_cols, hlocal_sem)
     hidden_local.start()
 
-    send("ay_r1", head_ref.at[0], out_ref.at[y, z, 0], dev(yr, z))
-    send("ay_l1", head_ref.at[0], out_ref.at[y, z, 0], dev(yl, z))
-    send("bz_r1", head_ref.at[1], out_ref.at[y, z, 1], dev(y, zs(1)))
-    send("bz_l1", head_ref.at[1], out_ref.at[y, z, 1], dev(y, zs(-1)))
-
-    zhalf = nz // 2
-    yhalf = ny // 2
-
-    def fwd_single_z(step):
-        src_r = zs(-(step - 1))
-        src_l = zs(step - 1)
-        if step < zhalf or nz % 2 == 1:
-            send(f"bz_r{step}", out_ref.at[y, src_r, 1], out_ref.at[y, src_r, 1], dev(y, zs(1)))
-            send(f"bz_l{step}", out_ref.at[y, src_l, 1], out_ref.at[y, src_l, 1], dev(y, zs(-1)))
-        else:
-            send(f"bz_r{step}", out_ref.at[y, src_r, 1, pl.ds(0, hr)],
-                 out_ref.at[y, src_r, 1, pl.ds(0, hr)], dev(y, zs(1)))
-            send(f"bz_l{step}", out_ref.at[y, src_l, 1, pl.ds(hr, hr)],
-                 out_ref.at[y, src_l, 1, pl.ds(hr, hr)], dev(y, zs(-1)))
-
-    def fwd_single_y(step):
-        src_r = ys(-(step - 1))
-        src_l = ys(step - 1)
-        if step < yhalf or ny % 2 == 1:
-            send(f"ay_r{step}", out_ref.at[src_r, z, 0], out_ref.at[src_r, z, 0], dev(yr, z))
-            send(f"ay_l{step}", out_ref.at[src_l, z, 0], out_ref.at[src_l, z, 0], dev(yl, z))
-        else:
-            send(f"ay_r{step}", out_ref.at[src_r, z, 0, pl.ds(0, hr)],
-                 out_ref.at[src_r, z, 0, pl.ds(0, hr)], dev(yr, z))
-            send(f"ay_l{step}", out_ref.at[src_l, z, 0, pl.ds(hr, hr)],
-                 out_ref.at[src_l, z, 0, pl.ds(hr, hr)], dev(yl, z))
-
-    def fwd_group_z(step):
-        src_r = zs(-(step - 1))
-        src_l = zs(step - 1)
-        if step < zhalf or nz % 2 == 1:
-            send(f"az_r{step}", out_ref.at[:, src_r, 0], out_ref.at[:, src_r, 0], dev(y, zs(1)))
-            send(f"az_l{step}", out_ref.at[:, src_l, 0], out_ref.at[:, src_l, 0], dev(y, zs(-1)))
-        else:
-            send(f"az_r{step}", out_ref.at[pl.ds(0, yhalf), src_r, 0],
-                 out_ref.at[pl.ds(0, yhalf), src_r, 0], dev(y, zs(1)))
-            send(f"az_l{step}", out_ref.at[pl.ds(yhalf, ny - yhalf), src_l, 0],
-                 out_ref.at[pl.ds(yhalf, ny - yhalf), src_l, 0], dev(y, zs(-1)))
-
-    def fwd_group_y(step):
-        src_r = ys(-(step - 1))
-        src_l = ys(step - 1)
-        if step < yhalf or ny % 2 == 1:
-            send(f"by_r{step}", out_ref.at[src_r, :, 1], out_ref.at[src_r, :, 1], dev(yr, z))
-            send(f"by_l{step}", out_ref.at[src_l, :, 1], out_ref.at[src_l, :, 1], dev(yl, z))
-        else:
-            send(f"by_r{step}", out_ref.at[src_r, pl.ds(0, zhalf), 1],
-                 out_ref.at[src_r, pl.ds(0, zhalf), 1], dev(yr, z))
-            send(f"by_l{step}", out_ref.at[src_l, pl.ds(zhalf, nz - zhalf), 1],
-                 out_ref.at[src_l, pl.ds(zhalf, nz - zhalf), 1], dev(yl, z))
-
-    ysteps = ny // 2 if ny % 2 == 0 else (ny - 1) // 2
-    zsteps = nz // 2 if nz % 2 == 0 else (nz - 1) // 2
-
-    for step in range(2, max(ysteps, zsteps) + 1):
-        if step <= ysteps:
-            arrived(f"ay_r{step - 1}")
-            arrived(f"ay_l{step - 1}")
-            fwd_single_y(step)
-        if step <= zsteps:
-            arrived(f"bz_r{step - 1}")
-            arrived(f"bz_l{step - 1}")
-            fwd_single_z(step)
+    plan = []
+
+    def ring_plan(name, n, block, right, left, first_src, needs0):
+        steps = n // 2
+        for step in range(1, steps + 1):
+            for side, peer, sign in (("r", right, -1), ("l", left, 1)):
+                key = f"{name}{side}{step}"
+                view = block(sign * (step - 1))
+                if 2 * step == n:
+                    view = view.at[pl.ds(0, hr)] if side == "r" else view.at[pl.ds(hr, rows - hr)]
+                    src = view
+                elif step == 1 and first_src is not None:
+                    src = first_src
+                else:
+                    src = view
+                if step == 1 and 2 * step == n and first_src is not None:
+                    src = first_src.at[pl.ds(0, hr)] if side == "r" else first_src.at[pl.ds(hr, rows - hr)]
+                needs = list(needs0) if step == 1 else [f"{name}{side}{step - 1}"]
+                plan.append((key, src, view, peer, needs))
+
+    right_y, left_y = dev(yr, z), dev(yl, z)
+    right_z, left_z = dev(y, zs(1)), dev(y, zs(-1))
+
+    def arrival_keys(name, n, offset):
+        steps = n // 2
+        if offset == 0:
+            return []
+        k = abs(offset) if abs(offset) <= steps else n - abs(offset)
+        if 2 * k == n:
+            return [f"{name}r{k}", f"{name}l{k}"]
+        return [f"{name}r{k}"] if offset < 0 else [f"{name}l{k}"]
+
+    ring_plan("ay", ny, lambda k: out_ref.at[ys(k), z, 0], right_y, left_y, head_ref.at[0], [])
+    ring_plan("bz", nz, lambda k: out_ref.at[y, zs(k), 1], right_z, left_z, head_ref.at[1], [])
+    y_offsets = [0] + [s * k for k in range(1, ny // 2 + 1) for s in (-1, 1) if not (s == 1 and 2 * k == ny)]
+    z_offsets = [0] + [s * k for k in range(1, nz // 2 + 1) for s in (-1, 1) if not (s == 1 and 2 * k == nz)]
+    for dy in y_offsets:
+        ring_plan(f"az{dy + ny}_", nz, lambda k, dy=dy: out_ref.at[ys(dy), zs(k), 0], right_z, left_z,
+                  head_ref.at[0] if dy == 0 else None, arrival_keys("ay", ny, dy))
+    for dz in z_offsets:
+        ring_plan(f"by{dz + nz}_", ny, lambda k, dz=dz: out_ref.at[ys(k), zs(dz), 1], right_y, left_y,
+                  head_ref.at[1] if dz == 0 else None, arrival_keys("bz", nz, dz))
+
+    level = {}
+    for key, _, _, _, needs in plan:
+        level[key] = 1 + max([level[n] for n in needs], default=-1)
+    order = sorted(range(len(plan)), key=lambda i: (level[plan[i][0]], i))
+    index = {plan[i][0]: i for i in range(len(plan))}
+    waited = set()
+    copies = {}
+    for i in order:
+        key, src, dst, peer, needs = plan[i]
+        for n in needs:
+            if n not in waited:
+                copies[n].wait_recv()
+                waited.add(n)
+        c = pltpu.make_async_remote_copy(
+            src_ref=src,
+            dst_ref=dst,
+            send_sem=send_sem.at[index[key]],
+            recv_sem=recv_sem.at[index[key]],
+            device_id=peer,
+            device_id_type=MESH,
+        )
+        c.start()
+        copies[key] = c
+    for i in order:
+        key = plan[i][0]
+        if key not in waited:
+            copies[key].wait_recv()
+            waited.add(key)
     local.wait()
-    if ysteps >= 1:
-        arrived(f"ay_r{ysteps}")
-        arrived(f"ay_l{ysteps}")
-    send("az_r1", out_ref.at[:, z, 0], out_ref.at[:, z, 0], dev(y, zs(1)))
-    send("az_l1", out_ref.at[:, z, 0], out_ref.at[:, z, 0], dev(y, zs(-1)))
-    if zsteps >= 1:
-        arrived(f"bz_r{zsteps}")
-        arrived(f"bz_l{zsteps}")
-    send("by_r1", out_ref.at[y, :, 1], out_ref.at[y, :, 1], dev(yr, z))
-    send("by_l1", out_ref.at[y, :, 1], out_ref.at[y, :, 1], dev(yl, z))
-    for step in range(2, max(ysteps, zsteps) + 1):
-        if step <= zsteps:
-            arrived(f"az_r{step - 1}")
-            arrived(f"az_l{step - 1}")
-            fwd_group_z(step)
-        if step <= ysteps:
-            arrived(f"by_r{step - 1}")
-            arrived(f"by_l{step - 1}")
-            fwd_group_y(step)
-    arrived(f"az_r{zsteps}")
-    arrived(f"az_l{zsteps}")
-    arrived(f"by_r{ysteps}")
-    arrived(f"by_l{ysteps}")
     hidden_local.wait()
     for c in hidden_copies:
         c.wait_recv()
@@ -189,7 +169,7 @@
     rows, width = head.shape
     slots, breadth = hidden.shape
     blocks = head.reshape(2, rows // 2, width)
-    streams = 4 * (ny // 2 + nz // 2)
+    streams = 2 * (ny // 2 + nz // 2 + ny * (nz // 2) + nz * (ny // 2))
     out, feat = pl.pallas_call(
         functools.partial(head_gather_kernel, ny, nz, nv),
         out_shape=(

time: 162 us -> 160 us (0.988)
  Pallas kernels: 126 us -> 123 us
    pallas_call x1, Pallas kernels: 14.5 us -> 9.39 us  [exchange_stats(): pl.pallas_call(functools.partial(stats_kernel, n), out_shape=jax.ShapeDty...]
    pallas_call x1, Pallas kernels: 112 us -> 114 us  [gather_all(): pl.pallas_call(functools.partial(head_gather_kernel, ny, nz, nv), out_sha...]
where the time goes in v7:
time: 160 us; the launch traced here: 159 us
  Pallas kernels  123 us (77%)
  matrix products  20.9 us (13%)
  other arithmetic  13.5 us (8%)
    pallas_call x1, Pallas kernels, gather_all(): pl.pallas_call(functools.partial(head_gather_kernel, ny, nz, nv), out_sha...  114 us
    dot_general x1, matrix products, local(): logits = jnp.dot(normed, columns, preferred_element_type=jnp.float32)  20.9 us
    pallas_call x1, Pallas kernels, exchange_stats(): pl.pallas_call(functools.partial(stats_kernel, n), out_shape=jax.ShapeDty...  9.39 us
    reduce_sum x1, other arithmetic, local(): total_local = jnp.sum(expo, axis=1)  6.99 us

profile of v7, /device:TPU:1, one launch (start us, length us, event | category | flops | bytes accessed | tf_op | source)
XLA Modules:
  0.0 159.3 jit_solution(5205190565590095754)
XLA Ops:
  0.6 114.1 %shard_map.77 = (bf16[4,8,2,32,4000]{4,3,2,1,0:T(8,128)(2,1)}, bf16[768,2048]{1,0:T(8,128)(2,1)}) custom-call(bf16[2,32,4000]{2,1,0:T(8,128)(2,1)} %bitcast.24, bf16[768,256]{1,0:T(8,128)(2,1)} %hidden_ref.1), custom_call_target="tpu_custom_call" | custom-call | bytes 32768000 | tf_op jit(solution)/shard_map/pallas_call | solution.py:173
  114.7 2.6 %fusion.1 = f32[768]{0:T(1024)S(1)} fusion(bf16[768,2048]{1,0:T(8,128)(2,1)} %get-tuple-element.4), kind=kLoop, calls=%fused_computation.7 | loop fusion | flops 4717824 | bytes 3148800 | tf_op jit(solution)/shard_map/reduce_sum | solution.py:251
  117.3 0.7 convert_element_type.10
  118.0 0.0 copy-start
  118.0 20.9 %fusion.14 = (f32[768]{0:T(1024)S(1)}, f32[768,4000]{0,1:T(8,128)}) fusion(bf16[2048,4000]{1,0:T(8,128)(2,1)} %bitcast.25, bf16[768,2048]{1,0:T(8,128)(2,1)} %get-tuple-element.4, f32[2048]{0:T(1024)S(1)} %convert_element_type.10, f32[768]{0:T(1024)S(1)} %add_rsqrt_fusion), kind=kOutput, calls=%fused_computation.33 | convolution fusion | flops 12592274432 | bytes 31832064 | tf_op jit(solution)/shard_map/dot_general | solution.py:254
  138.9 0.0 copy-start.1
  138.9 0.0 copy-start.2
  138.9 0.0 copy-done
  138.9 7.0 %fusion = (f32[768]{0:T(1024)S(1)}, f32[768]{0:T(1024)S(1)}, f32[768]{0:T(1024)S(1)}) fusion(f32[768,4000]{0,1:T(8,128)} %get-tuple-element.21, f32[768]{0:T(1024)S(1)} %get-tuple-element.20, s32[768]{0:T(1024)S(1)} %broadcast_subtract_fusion), kind=kLoop, calls=%fused_computation.4 | loop fusion | flops 21501696 | bytes 12303360 | tf_op jit(solution)/shard_map/reduce_sum | solution.py:257
  145.9 0.6 pad_maximum_fusion.stats_ref
  146.6 9.4 %shard_map.78 = f32[8,4,768]{2,1,0:T(4,128)} custom-call(f32[4,768]{1,0:T(4,128)} %pad_maximum_fusion.stats_ref), custom_call_target="tpu_custom_call" | custom-call | tf_op jit(solution)/shard_map/pallas_call | solution.py:224
  156.0 1.2 fusion.13
  157.2 0.0 copy-done.1
  157.2 0.0 copy-done.2
  157.2 0.1 select_reduce_fusion.1
  157.3 0.7 dynamic_slice.3
  158.0 1.3 subtract_select_fusion
  (7 shorter events, 0.1 us)
Async XLA Ops:
  118.0 20.9 %copy-start = (s32[768]{0:T(1024)S(1)}, s32[768]{0:T(1024)}, u32[]{:S(2)}) copy-start(s32[768]{0:T(1024)} %param.9) | copy-start | bytes 9220
  138.9 18.3 %copy-start.1 = (s32[64]{0:T(128)S(1)}, s32[64]{0:T(128)}, u32[]{:S(2)}) copy-start(s32[64]{0:T(128)} %param.10) | copy-start | bytes 772
  138.9 18.3 %copy-start.2 = (s32[64]{0:T(128)S(1)}, s32[64]{0:T(128)}, u32[]{:S(2)}) copy-start(s32[64]{0:T(128)} %param.11) | copy-start | bytes 772

commit v8 on v7

--- a/solution.py
+++ b/solution.py
@@ -21,7 +21,7 @@
     return size // nz, nz
 
 
-def head_gather_kernel(ny, nz, nv, head_ref, hidden_ref, out_ref, feat_ref, send_sem, recv_sem,
+def head_gather_kernel(ny, nz, nv, split, head_ref, hidden_ref, out_ref, feat_ref, send_sem, recv_sem,
                        local_sem, hsend_sem, hrecv_sem, hlocal_sem):
     dp = lax.axis_index("dp")
     v = lax.axis_index("vocab")
@@ -39,8 +39,9 @@
     def dev(yy, zz):
         return (yy * nz + zz, v)
 
-    rows = head_ref.shape[1]
+    rows, width = head_ref.shape
     hr = rows // 2
+    cols = (pl.ds(0, split), pl.ds(split, width - split))
 
     barrier = pltpu.get_barrier_semaphore()
     peers = [dev(yr, z), dev(yl, z), dev(y, zs(1)), dev(y, zs(-1))]
@@ -118,16 +119,20 @@
             return [f"{name}r{k}", f"{name}l{k}"]
         return [f"{name}r{k}"] if offset < 0 else [f"{name}l{k}"]
 
-    ring_plan("ay", ny, lambda k: out_ref.at[ys(k), z, 0], right_y, left_y, head_ref.at[0], [])
-    ring_plan("bz", nz, lambda k: out_ref.at[y, zs(k), 1], right_z, left_z, head_ref.at[1], [])
+    ring_plan("ay", ny, lambda k: out_ref.at[ys(k), z, :, cols[0]], right_y, left_y,
+              head_ref.at[:, cols[0]], [])
+    ring_plan("bz", nz, lambda k: out_ref.at[y, zs(k), :, cols[1]], right_z, left_z,
+              head_ref.at[:, cols[1]], [])
     y_offsets = [0] + [s * k for k in range(1, ny // 2 + 1) for s in (-1, 1) if not (s == 1 and 2 * k == ny)]
     z_offsets = [0] + [s * k for k in range(1, nz // 2 + 1) for s in (-1, 1) if not (s == 1 and 2 * k == nz)]
     for dy in y_offsets:
-        ring_plan(f"az{dy + ny}_", nz, lambda k, dy=dy: out_ref.at[ys(dy), zs(k), 0], right_z, left_z,
-                  head_ref.at[0] if dy == 0 else None, arrival_keys("ay", ny, dy))
+        ring_plan(f"az{dy + ny}_", nz, lambda k, dy=dy: out_ref.at[ys(dy), zs(k), :, cols[0]],
+                  right_z, left_z, head_ref.at[:, cols[0]] if dy == 0 else None,
+                  arrival_keys("ay", ny, dy))
     for dz in z_offsets:
-        ring_plan(f"by{dz + nz}_", ny, lambda k, dz=dz: out_ref.at[ys(k), zs(dz), 1], right_y, left_y,
-                  head_ref.at[1] if dz == 0 else None, arrival_keys("bz", nz, dz))
+        ring_plan(f"by{dz + nz}_", ny, lambda k, dz=dz: out_ref.at[ys(k), zs(dz), :, cols[1]],
+                  right_y, left_y, head_ref.at[:, cols[1]] if dz == 0 else None,
+                  arrival_keys("bz", nz, dz))
 
     level = {}
     for key, _, _, _, needs in plan:
@@ -168,12 +173,12 @@
 def gather_all(head, hidden, ny, nz, nv):
     rows, width = head.shape
     slots, breadth = hidden.shape
-    blocks = head.reshape(2, rows // 2, width)
+    split = max(128, min(width - 128, int(round(width * 0.405 / 128)) * 128))
     streams = 2 * (ny // 2 + nz // 2 + ny * (nz // 2) + nz * (ny // 2))
     out, feat = pl.pallas_call(
-        functools.partial(head_gather_kernel, ny, nz, nv),
+        functools.partial(head_gather_kernel, ny, nz, nv, split),
         out_shape=(
-            jax.ShapeDtypeStruct((ny, nz, 2, rows // 2, width), head.dtype),
+            jax.ShapeDtypeStruct((ny, nz, rows, width), head.dtype),
             jax.ShapeDtypeStruct((slots, nv * breadth), hidden.dtype),
         ),
         in_specs=[pl.BlockSpec(memory_space=pl.ANY)] * 2,
@@ -190,7 +195,7 @@
         cost_estimate=pl.CostEstimate(
             flops=0, transcendentals=0, bytes_accessed=2 * ny * nz * rows * width * 2
         ),
-    )(blocks, hidden)
+    )(head, hidden)
     return out.reshape(ny * nz * rows, width), feat
 
 

time: 160 us -> 154 us (0.963)
  Pallas kernels: 123 us -> 118 us
    pallas_call x1, Pallas kernels: 114 us -> 110 us  [gather_all(): pl.pallas_call(functools.partial(head_gather_kernel, ny, nz, nv, split),...]
where the time goes in v8:
time: 154 us
  Pallas kernels  118 us (77%)
  matrix products  20.9 us (14%)
  other arithmetic  13.5 us (9%)
    pallas_call x1, Pallas kernels, gather_all(): pl.pallas_call(functools.partial(head_gather_kernel, ny, nz, nv, split),...  110 us
    dot_general x1, matrix products, local(): logits = jnp.dot(normed, columns, preferred_element_type=jnp.float32)  20.9 us
    pallas_call x1, Pallas kernels, exchange_stats(): pl.pallas_call(functools.partial(stats_kernel, n), out_shape=jax.ShapeDty...  8.45 us
    reduce_sum x1, other arithmetic, local(): total_local = jnp.sum(expo, axis=1)  6.99 us

profile of v8, /device:TPU:1, one launch (start us, length us, event | category | flops | bytes accessed | tf_op | source)
XLA Modules:
  0.0 154.1 jit_solution(6132419110989372910)
XLA Ops:
  0.6 109.8 %shard_map.77 = (bf16[4,8,64,4000]{3,2,1,0:T(8,128)(2,1)}, bf16[768,2048]{1,0:T(8,128)(2,1)}) custom-call(bf16[64,4000]{1,0:T(8,128)(2,1)} %head_ref.1, bf16[768,256]{1,0:T(8,128)(2,1)} %hidden_ref.1), custom_call_target="tpu_custom_call" | custom-call | bytes 32768000 | tf_op jit(solution)/shard_map/pallas_call | solution.py:178
  110.5 2.6 %fusion.1 = f32[768]{0:T(1024)S(1)} fusion(bf16[768,2048]{1,0:T(8,128)(2,1)} %get-tuple-element.4), kind=kLoop, calls=%fused_computation.7 | loop fusion | flops 4717824 | bytes 3148800 | tf_op jit(solution)/shard_map/reduce_sum | solution.py:256
  113.1 0.7 convert_element_type.10
  113.8 0.0 copy-start
  113.8 20.9 %fusion.14 = (f32[768]{0:T(1024)S(1)}, f32[768,4000]{0,1:T(8,128)}) fusion(bf16[2048,4000]{1,0:T(8,128)(2,1)} %bitcast.23, bf16[768,2048]{1,0:T(8,128)(2,1)} %get-tuple-element.4, f32[2048]{0:T(1024)S(1)} %convert_element_type.10, f32[768]{0:T(1024)S(1)} %add_rsqrt_fusion), kind=kOutput, calls=%fused_computation.33 | convolution fusion | flops 12592274432 | bytes 31832064 | tf_op jit(solution)/shard_map/dot_general | solution.py:259
  134.7 0.0 copy-start.1
  134.7 0.0 copy-start.2
  134.7 0.0 copy-done
  134.7 7.0 %fusion = (f32[768]{0:T(1024)S(1)}, f32[768]{0:T(1024)S(1)}, f32[768]{0:T(1024)S(1)}) fusion(f32[768,4000]{0,1:T(8,128)} %get-tuple-element.21, f32[768]{0:T(1024)S(1)} %get-tuple-element.20, s32[768]{0:T(1024)S(1)} %broadcast_subtract_fusion), kind=kLoop, calls=%fused_computation.4 | loop fusion | flops 21501696 | bytes 12303360 | tf_op jit(solution)/shard_map/reduce_sum | solution.py:262
  141.7 0.6 pad_maximum_fusion.stats_ref
  142.3 8.5 %shard_map.78 = f32[8,4,768]{2,1,0:T(4,128)} custom-call(f32[4,768]{1,0:T(4,128)} %pad_maximum_fusion.stats_ref), custom_call_target="tpu_custom_call" | custom-call | tf_op jit(solution)/shard_map/pallas_call | solution.py:229
  150.8 1.2 fusion.13
  152.0 0.0 copy-done.1
  152.0 0.0 copy-done.2
  152.1 0.1 select_reduce_fusion.1
  152.2 0.7 dynamic_slice.3
  152.8 1.3 subtract_select_fusion
  (7 shorter events, 0.1 us)
Async XLA Ops:
  113.8 20.9 %copy-start = (s32[768]{0:T(1024)S(1)}, s32[768]{0:T(1024)}, u32[]{:S(2)}) copy-start(s32[768]{0:T(1024)} %param.9) | copy-start | bytes 9220
  134.7 17.4 %copy-start.1 = (s32[64]{0:T(128)S(1)}, s32[64]{0:T(128)}, u32[]{:S(2)}) copy-start(s32[64]{0:T(128)} %param.10) | copy-start | bytes 772
  134.7 17.4 %copy-start.2 = (s32[64]{0:T(128)S(1)}, s32[64]{0:T(128)}, u32[]{:S(2)}) copy-start(s32[64]{0:T(128)} %param.11) | copy-start | bytes 772

commit v9 on v8

--- a/solution.py
+++ b/solution.py
@@ -39,8 +39,10 @@
     def dev(yy, zz):
         return (yy * nz + zz, v)
 
-    rows, width = head_ref.shape
-    hr = rows // 2
+    width = head_ref.shape[1]
+    parts = 2
+    prow = head_ref.shape[0] // parts
+    rows, hr = prow, prow // 2
     cols = (pl.ds(0, split), pl.ds(split, width - split))
 
     barrier = pltpu.get_barrier_semaphore()
@@ -119,20 +121,24 @@
             return [f"{name}r{k}", f"{name}l{k}"]
         return [f"{name}r{k}"] if offset < 0 else [f"{name}l{k}"]
 
-    ring_plan("ay", ny, lambda k: out_ref.at[ys(k), z, :, cols[0]], right_y, left_y,
-              head_ref.at[:, cols[0]], [])
-    ring_plan("bz", nz, lambda k: out_ref.at[y, zs(k), :, cols[1]], right_z, left_z,
-              head_ref.at[:, cols[1]], [])
     y_offsets = [0] + [s * k for k in range(1, ny // 2 + 1) for s in (-1, 1) if not (s == 1 and 2 * k == ny)]
     z_offsets = [0] + [s * k for k in range(1, nz // 2 + 1) for s in (-1, 1) if not (s == 1 and 2 * k == nz)]
-    for dy in y_offsets:
-        ring_plan(f"az{dy + ny}_", nz, lambda k, dy=dy: out_ref.at[ys(dy), zs(k), :, cols[0]],
-                  right_z, left_z, head_ref.at[:, cols[0]] if dy == 0 else None,
-                  arrival_keys("ay", ny, dy))
-    for dz in z_offsets:
-        ring_plan(f"by{dz + nz}_", ny, lambda k, dz=dz: out_ref.at[ys(k), zs(dz), :, cols[1]],
-                  right_y, left_y, head_ref.at[:, cols[1]] if dz == 0 else None,
-                  arrival_keys("bz", nz, dz))
+    for q in range(parts):
+        rq = pl.ds(q * prow, prow)
+        ring_plan(f"ay{q}", ny, lambda k: out_ref.at[ys(k), z, rq, cols[0]], right_y, left_y,
+                  head_ref.at[rq, cols[0]], [])
+        ring_plan(f"bz{q}", nz, lambda k: out_ref.at[y, zs(k), rq, cols[1]], right_z, left_z,
+                  head_ref.at[rq, cols[1]], [])
+        for dy in y_offsets:
+            ring_plan(f"az{q}.{dy + ny}_", nz,
+                      lambda k, dy=dy: out_ref.at[ys(dy), zs(k), rq, cols[0]],
+                      right_z, left_z, head_ref.at[rq, cols[0]] if dy == 0 else None,
+                      arrival_keys(f"ay{q}", ny, dy))
+        for dz in z_offsets:
+            ring_plan(f"by{q}.{dz + nz}_", ny,
+                      lambda k, dz=dz: out_ref.at[ys(k), zs(dz), rq, cols[1]],
+                      right_y, left_y, head_ref.at[rq, cols[1]] if dz == 0 else None,
+                      arrival_keys(f"bz{q}", nz, dz))
 
     level = {}
     for key, _, _, _, needs in plan:
@@ -174,7 +180,7 @@
     rows, width = head.shape
     slots, breadth = hidden.shape
     split = max(128, min(width - 128, int(round(width * 0.405 / 128)) * 128))
-    streams = 2 * (ny // 2 + nz // 2 + ny * (nz // 2) + nz * (ny // 2))
+    streams = 4 * (ny // 2 + nz // 2 + ny * (nz // 2) + nz * (ny // 2))
     out, feat = pl.pallas_call(
         functools.partial(head_gather_kernel, ny, nz, nv, split),
         out_shape=(

time: 154 us -> 149 us (0.968)
  Pallas kernels: 118 us -> 113 us
    pallas_call x1, Pallas kernels: 110 us -> 104 us  [gather_all(): pl.pallas_call(functools.partial(head_gather_kernel, ny, nz, nv, split),...]
where the time goes in v9:
time: 149 us
  Pallas kernels  113 us (76%)
  matrix products  20.9 us (14%)
  other arithmetic  13.5 us (9%)
    pallas_call x1, Pallas kernels, gather_all(): pl.pallas_call(functools.partial(head_gather_kernel, ny, nz, nv, split),...  104 us
    dot_general x1, matrix products, local(): logits = jnp.dot(normed, columns, preferred_element_type=jnp.float32)  20.9 us
    pallas_call x1, Pallas kernels, exchange_stats(): pl.pallas_call(functools.partial(stats_kernel, n), out_shape=jax.ShapeDty...  8.75 us
    reduce_sum x1, other arithmetic, local(): total_local = jnp.sum(expo, axis=1)  6.99 us

profile of v9, /device:TPU:1, one launch (start us, length us, event | category | flops | bytes accessed | tf_op | source)
XLA Modules:
  0.0 148.6 jit_solution(6100109215853061490)
XLA Ops:
  0.6 104.0 %shard_map.77 = (bf16[4,8,64,4000]{3,2,1,0:T(8,128)(2,1)}, bf16[768,2048]{1,0:T(8,128)(2,1)}) custom-call(bf16[64,4000]{1,0:T(8,128)(2,1)} %head_ref.1, bf16[768,256]{1,0:T(8,128)(2,1)} %hidden_ref.1), custom_call_target="tpu_custom_call" | custom-call | bytes 32768000 | tf_op jit(solution)/shard_map/pallas_call | solution.py:184
  104.6 2.6 %fusion.1 = f32[768]{0:T(1024)S(1)} fusion(bf16[768,2048]{1,0:T(8,128)(2,1)} %get-tuple-element.4), kind=kLoop, calls=%fused_computation.7 | loop fusion | flops 4717824 | bytes 3148800 | tf_op jit(solution)/shard_map/reduce_sum | solution.py:262
  107.2 0.7 convert_element_type.10
  107.9 0.0 copy-start
  107.9 20.9 %fusion.14 = (f32[768]{0:T(1024)S(1)}, f32[768,4000]{0,1:T(8,128)}) fusion(bf16[2048,4000]{1,0:T(8,128)(2,1)} %bitcast.23, bf16[768,2048]{1,0:T(8,128)(2,1)} %get-tuple-element.4, f32[2048]{0:T(1024)S(1)} %convert_element_type.10, f32[768]{0:T(1024)S(1)} %add_rsqrt_fusion), kind=kOutput, calls=%fused_computation.33 | convolution fusion | flops 12592274432 | bytes 31832064 | tf_op jit(solution)/shard_map/dot_general | solution.py:265
  128.8 0.0 copy-start.1
  128.8 0.0 copy-start.2
  128.8 0.0 copy-done
  128.8 7.0 %fusion = (f32[768]{0:T(1024)S(1)}, f32[768]{0:T(1024)S(1)}, f32[768]{0:T(1024)S(1)}) fusion(f32[768,4000]{0,1:T(8,128)} %get-tuple-element.21, f32[768]{0:T(1024)S(1)} %get-tuple-element.20, s32[768]{0:T(1024)S(1)} %broadcast_subtract_fusion), kind=kLoop, calls=%fused_computation.4 | loop fusion | flops 21501696 | bytes 12303360 | tf_op jit(solution)/shard_map/reduce_sum | solution.py:268
  135.9 0.6 pad_maximum_fusion.stats_ref
  136.5 8.7 %shard_map.78 = f32[8,4,768]{2,1,0:T(4,128)} custom-call(f32[4,768]{1,0:T(4,128)} %pad_maximum_fusion.stats_ref), custom_call_target="tpu_custom_call" | custom-call | tf_op jit(solution)/shard_map/pallas_call | solution.py:235
  145.3 1.2 fusion.13
  146.5 0.0 copy-done.1
  146.5 0.0 copy-done.2
  146.5 0.1 select_reduce_fusion.1
  146.6 0.7 dynamic_slice.3
  147.3 1.3 subtract_select_fusion
  (7 shorter events, 0.1 us)
Async XLA Ops:
  107.9 20.9 %copy-start = (s32[768]{0:T(1024)S(1)}, s32[768]{0:T(1024)}, u32[]{:S(2)}) copy-start(s32[768]{0:T(1024)} %param.9) | copy-start | bytes 9220
  128.8 17.7 %copy-start.1 = (s32[64]{0:T(128)S(1)}, s32[64]{0:T(128)}, u32[]{:S(2)}) copy-start(s32[64]{0:T(128)} %param.10) | copy-start | bytes 772
  128.8 17.7 %copy-start.2 = (s32[64]{0:T(128)S(1)}, s32[64]{0:T(128)}, u32[]{:S(2)}) copy-start(s32[64]{0:T(128)} %param.11) | copy-start | bytes 772

commit v10 on v9

--- a/solution.py
+++ b/solution.py
@@ -40,7 +40,7 @@
         return (yy * nz + zz, v)
 
     width = head_ref.shape[1]
-    parts = 2
+    parts = 4
     prow = head_ref.shape[0] // parts
     rows, hr = prow, prow // 2
     cols = (pl.ds(0, split), pl.ds(split, width - split))
@@ -97,7 +97,11 @@
             for side, peer, sign in (("r", right, -1), ("l", left, 1)):
                 key = f"{name}{side}{step}"
                 view = block(sign * (step - 1))
-                if 2 * step == n:
+                if 2 * step == n and opp != "split":
+                    if side != opp:
+                        continue
+                    src = first_src if (step == 1 and first_src is not None) else view
+                elif 2 * step == n:
                     view = view.at[pl.ds(0, hr)] if side == "r" else view.at[pl.ds(hr, rows - hr)]
                     src = view
                 elif step == 1 and first_src is not None:
@@ -118,13 +122,14 @@
             return []
         k = abs(offset) if abs(offset) <= steps else n - abs(offset)
         if 2 * k == n:
-            return [f"{name}r{k}", f"{name}l{k}"]
+            return [f"{name}r{k}", f"{name}l{k}"] if opp == "split" else [f"{name}{opp}{k}"]
         return [f"{name}r{k}"] if offset < 0 else [f"{name}l{k}"]
 
     y_offsets = [0] + [s * k for k in range(1, ny // 2 + 1) for s in (-1, 1) if not (s == 1 and 2 * k == ny)]
     z_offsets = [0] + [s * k for k in range(1, nz // 2 + 1) for s in (-1, 1) if not (s == 1 and 2 * k == nz)]
     for q in range(parts):
         rq = pl.ds(q * prow, prow)
+        opp = "r" if q % 2 == 0 else "l"
         ring_plan(f"ay{q}", ny, lambda k: out_ref.at[ys(k), z, rq, cols[0]], right_y, left_y,
                   head_ref.at[rq, cols[0]], [])
         ring_plan(f"bz{q}", nz, lambda k: out_ref.at[y, zs(k), rq, cols[1]], right_z, left_z,
@@ -180,7 +185,7 @@
     rows, width = head.shape
     slots, breadth = hidden.shape
     split = max(128, min(width - 128, int(round(width * 0.405 / 128)) * 128))
-    streams = 4 * (ny // 2 + nz // 2 + ny * (nz // 2) + nz * (ny // 2))
+    streams = 8 * (ny // 2 + nz // 2 + ny * (nz // 2) + nz * (ny // 2))
     out, feat = pl.pallas_call(
         functools.partial(head_gather_kernel, ny, nz, nv, split),
         out_shape=(

time: 149 us -> 151 us (1.013)
    pallas_call x1, Pallas kernels: 104 us -> 106 us  [gather_all(): pl.pallas_call(functools.partial(head_gather_kernel, ny, nz, nv, split),...]
where the time goes in v10:
time: 151 us; the launch traced here: 150 us
  Pallas kernels  114 us (75%)
  matrix products  20.9 us (14%)
  other arithmetic  13.5 us (9%)
    pallas_call x1, Pallas kernels, gather_all(): pl.pallas_call(functools.partial(head_gather_kernel, ny, nz, nv, split),...  106 us
    dot_general x1, matrix products, local(): logits = jnp.dot(normed, columns, preferred_element_type=jnp.float32)  20.9 us
    pallas_call x1, Pallas kernels, exchange_stats(): pl.pallas_call(functools.partial(stats_kernel, n), out_shape=jax.ShapeDty...  8.75 us
    reduce_sum x1, other arithmetic, local(): total_local = jnp.sum(expo, axis=1)  6.99 us

profile of v10, /device:TPU:1, one launch (start us, length us, event | category | flops | bytes accessed | tf_op | source)
XLA Modules:
  0.0 150.3 jit_solution(6616060591254323966)
XLA Ops:
  0.6 105.7 %shard_map.77 = (bf16[4,8,64,4000]{3,2,1,0:T(8,128)(2,1)}, bf16[768,2048]{1,0:T(8,128)(2,1)}) custom-call(bf16[64,4000]{1,0:T(8,128)(2,1)} %head_ref.1, bf16[768,256]{1,0:T(8,128)(2,1)} %hidden_ref.1), custom_call_target="tpu_custom_call" | custom-call | bytes 32768000 | tf_op jit(solution)/shard_map/pallas_call | solution.py:189
  106.4 2.6 %fusion.1 = f32[768]{0:T(1024)S(1)} fusion(bf16[768,2048]{1,0:T(8,128)(2,1)} %get-tuple-element.4), kind=kLoop, calls=%fused_computation.7 | loop fusion | flops 4717824 | bytes 3148800 | tf_op jit(solution)/shard_map/reduce_sum | solution.py:267
  109.0 0.7 convert_element_type.10
  109.6 0.0 copy-start
  109.6 20.9 %fusion.14 = (f32[768]{0:T(1024)S(1)}, f32[768,4000]{0,1:T(8,128)}) fusion(bf16[2048,4000]{1,0:T(8,128)(2,1)} %bitcast.23, bf16[768,2048]{1,0:T(8,128)(2,1)} %get-tuple-element.4, f32[2048]{0:T(1024)S(1)} %convert_element_type.10, f32[768]{0:T(1024)S(1)} %add_rsqrt_fusion), kind=kOutput, calls=%fused_computation.33 | convolution fusion | flops 12592274432 | bytes 31832064 | tf_op jit(solution)/shard_map/dot_general | solution.py:270
  130.6 0.0 copy-start.1
  130.6 0.0 copy-start.2
  130.6 0.0 copy-done
  130.6 7.0 %fusion = (f32[768]{0:T(1024)S(1)}, f32[768]{0:T(1024)S(1)}, f32[768]{0:T(1024)S(1)}) fusion(f32[768,4000]{0,1:T(8,128)} %get-tuple-element.21, f32[768]{0:T(1024)S(1)} %get-tuple-element.20, s32[768]{0:T(1024)S(1)} %broadcast_subtract_fusion), kind=kLoop, calls=%fused_computation.4 | loop fusion | flops 21501696 | bytes 12303360 | tf_op jit(solution)/shard_map/reduce_sum | solution.py:273
  137.6 0.6 pad_maximum_fusion.stats_ref
  138.2 8.8 %shard_map.78 = f32[8,4,768]{2,1,0:T(4,128)} custom-call(f32[4,768]{1,0:T(4,128)} %pad_maximum_fusion.stats_ref), custom_call_target="tpu_custom_call" | custom-call | tf_op jit(solution)/shard_map/pallas_call | solution.py:240
  147.0 1.2 fusion.13
  148.2 0.0 copy-done.1
  148.2 0.0 copy-done.2
  148.3 0.1 select_reduce_fusion.1
  148.4 0.7 dynamic_slice.3
  149.0 1.3 subtract_select_fusion
  (7 shorter events, 0.1 us)
Async XLA Ops:
  109.6 20.9 %copy-start = (s32[768]{0:T(1024)S(1)}, s32[768]{0:T(1024)}, u32[]{:S(2)}) copy-start(s32[768]{0:T(1024)} %param.9) | copy-start | bytes 9220
  130.6 17.7 %copy-start.1 = (s32[64]{0:T(128)S(1)}, s32[64]{0:T(128)}, u32[]{:S(2)}) copy-start(s32[64]{0:T(128)} %param.10) | copy-start | bytes 772
  130.6 17.7 %copy-start.2 = (s32[64]{0:T(128)S(1)}, s32[64]{0:T(128)}, u32[]{:S(2)}) copy-start(s32[64]{0:T(128)} %param.11) | copy-start | bytes 772

commit v11 on v9

--- a/solution.py
+++ b/solution.py
@@ -21,8 +21,8 @@
     return size // nz, nz
 
 
-def head_gather_kernel(ny, nz, nv, split, head_ref, hidden_ref, out_ref, feat_ref, send_sem, recv_sem,
-                       local_sem, hsend_sem, hrecv_sem, hlocal_sem):
+def head_gather_kernel(ny, nz, nv, split, head_ref, hidden_ref, gain_ref, out_ref, normed_ref,
+                       send_sem, recv_sem, local_sem, hsend_sem, hrecv_sem, hlocal_sem, feat_ref):
     dp = lax.axis_index("dp")
     v = lax.axis_index("vocab")
     y = dp // nz
@@ -163,32 +163,42 @@
         )
         c.start()
         copies[key] = c
+    hidden_local.wait()
+    for c in hidden_copies:
+        c.wait_recv()
+    tile = 64
+
+    def norm_rows(i, carry):
+        r = pl.ds(pl.multiple_of(i * tile, tile), tile)
+        wide = feat_ref[r, :].astype(jnp.float32)
+        scale = lax.rsqrt(jnp.mean(wide * wide, axis=1, keepdims=True) + EPS)
+        normed_ref[r, :] = (wide * scale * gain_ref[...]).astype(normed_ref.dtype)
+        return carry
+
+    lax.fori_loop(0, feat_ref.shape[0] // tile, norm_rows, 0)
     for i in order:
         key = plan[i][0]
         if key not in waited:
             copies[key].wait_recv()
             waited.add(key)
     local.wait()
-    hidden_local.wait()
-    for c in hidden_copies:
-        c.wait_recv()
     for c in list(copies.values()) + hidden_copies:
         c.wait_send()
 
 
-def gather_all(head, hidden, ny, nz, nv):
+def gather_all(head, hidden, gain, ny, nz, nv):
     rows, width = head.shape
     slots, breadth = hidden.shape
     split = max(128, min(width - 128, int(round(width * 0.405 / 128)) * 128))
     streams = 4 * (ny // 2 + nz // 2 + ny * (nz // 2) + nz * (ny // 2))
-    out, feat = pl.pallas_call(
+    out, normed = pl.pallas_call(
         functools.partial(head_gather_kernel, ny, nz, nv, split),
         out_shape=(
             jax.ShapeDtypeStruct((ny, nz, rows, width), head.dtype),
             jax.ShapeDtypeStruct((slots, nv * breadth), hidden.dtype),
         ),
-        in_specs=[pl.BlockSpec(memory_space=pl.ANY)] * 2,
-        out_specs=(pl.BlockSpec(memory_space=pl.ANY),) * 2,
+        in_specs=[pl.BlockSpec(memory_space=pl.ANY)] * 2 + [pl.BlockSpec(memory_space=pltpu.VMEM)],
+        out_specs=(pl.BlockSpec(memory_space=pl.ANY), pl.BlockSpec(memory_space=pltpu.VMEM)),
         scratch_shapes=[
             pltpu.SemaphoreType.DMA((streams,)),
             pltpu.SemaphoreType.DMA((streams,)),
@@ -196,13 +206,14 @@
             pltpu.SemaphoreType.DMA((nv - 1,)),
             pltpu.SemaphoreType.DMA((nv - 1,)),
             pltpu.SemaphoreType.DMA(()),
+            pltpu.VMEM((slots, nv * breadth), hidden.dtype),
         ],
         compiler_params=pltpu.CompilerParams(collective_id=0, has_side_effects=True),
         cost_estimate=pl.CostEstimate(
             flops=0, transcendentals=0, bytes_accessed=2 * ny * nz * rows * width * 2
         ),
-    )(head, hidden)
-    return out.reshape(ny * nz * rows, width), feat
+    )(head, hidden, gain.astype(jnp.float32).reshape(1, nv * breadth))
+    return out.reshape(ny * nz * rows, width), normed
 
 
 def stats_kernel(n, stats_ref, out_ref, send_sem, recv_sem):
@@ -255,13 +266,7 @@
     owners = jnp.arange(groups, dtype=jnp.int32)
     loads = jnp.sum(jnp.where(seq_owner[:, None] == owners[None, :], seq_lens[:, None], 0), axis=0)
     own_live = jnp.arange(slots, dtype=jnp.int32) < loads[position]
-    columns, features = gather_all(head, hidden, ny, nz, slices)
-    wide = features.astype(jnp.float32)
-    normed = (
-        wide
-        * lax.rsqrt(jnp.mean(wide * wide, axis=1, keepdims=True) + EPS)
-        * gain.astype(jnp.float32)
-    ).astype(jnp.bfloat16)
+    columns, normed = gather_all(head, hidden, gain, ny, nz, slices)
     logits = jnp.dot(normed, columns, preferred_element_type=jnp.float32)
     top_local = jnp.max(logits, axis=1)
     expo = jnp.exp(logits - top_local[:, None])

time: 149 us -> 148 us (level)
  Pallas kernels: 113 us -> 115 us
  other arithmetic: 13.5 us -> 11.5 us
    reduce_sum x1 -> x0, other arithmetic: 2.57 us -> none  [local(): jnp.mean(wide * wide, axis=1, keepdims=True) + EPS]
    pallas_call x1, Pallas kernels: 104 us -> 106 us  [gather_all(): pl.pallas_call(functools.partial(head_gather_kernel, ny, nz, nv, split),...]
where the time goes in v11:
time: 148 us
  Pallas kernels  115 us (78%)
  matrix products  20.4 us (14%)
  other arithmetic  11.5 us (8%)
    pallas_call x1, Pallas kernels, gather_all(): pl.pallas_call(functools.partial(head_gather_kernel, ny, nz, nv, split),...  106 us
    dot_general x1, matrix products, local(): logits = jnp.dot(normed, columns, preferred_element_type=jnp.float32)  20.4 us
    pallas_call x1, Pallas kernels, exchange_stats(): pl.pallas_call(functools.partial(stats_kernel, n), out_shape=jax.ShapeDty...  8.75 us
    reduce_sum x1, other arithmetic, local(): total_local = jnp.sum(expo, axis=1)  6.99 us

profile of v11, /device:TPU:1, one launch (start us, length us, event | category | flops | bytes accessed | tf_op | source)
XLA Modules:
  0.0 148.2 jit_solution(18283899618320047053)
XLA Ops:
  0.6 1.3 reshape.20
  1.9 106.1 %shard_map.77 = (bf16[4,8,64,4000]{3,2,1,0:T(8,128)(2,1)}, bf16[768,2048]{1,0:T(8,128)(2,1)}) custom-call(bf16[64,4000]{1,0:T(8,128)(2,1)} %head_ref.1, bf16[768,256]{1,0:T(8,128)(2,1)} %hidden_ref.1, f32[1,2048]{1,0:T(1,128)} %bitcast.25), custom_call_target="tpu_custom_call" | custom-call | bytes 32768000 | tf_op jit(solution)/shard_map/pallas_call | solution.py:194
  108.0 0.0 copy-start
  108.0 20.4 %fusion.7 = (f32[768]{0:T(1024)S(1)}, f32[768,4000]{0,1:T(8,128)}) fusion(bf16[768,2048]{1,0:T(8,128)(2,1)} %get-tuple-element.4, bf16[2048,4000]{1,0:T(8,128)(2,1)} %bitcast.26), kind=kOutput, calls=%fused_computation.24 | convolution fusion | flops 12585982976 | bytes 31820800 | tf_op jit(solution)/shard_map/dot_general | solution.py:270
  128.4 0.0 copy-start.1
  128.4 0.0 copy-start.2
  128.4 0.0 copy-done
  128.5 7.0 %fusion = (f32[768]{0:T(1024)S(1)}, f32[768]{0:T(1024)S(1)}, f32[768]{0:T(1024)S(1)}) fusion(f32[768,4000]{0,1:T(8,128)} %get-tuple-element.21, f32[768]{0:T(1024)S(1)} %get-tuple-element.20, s32[768]{0:T(1024)S(1)} %broadcast_subtract_fusion), kind=kLoop, calls=%fused_computation.4 | loop fusion | flops 21501696 | bytes 12303360 | tf_op jit(solution)/shard_map/reduce_sum | solution.py:273
  135.5 0.6 pad_maximum_fusion.stats_ref
  136.1 8.7 %shard_map.78 = f32[8,4,768]{2,1,0:T(4,128)} custom-call(f32[4,768]{1,0:T(4,128)} %pad_maximum_fusion.stats_ref), custom_call_target="tpu_custom_call" | custom-call | tf_op jit(solution)/shard_map/pallas_call | solution.py:246
  144.9 1.2 fusion.6
  146.1 0.0 copy-done.1
  146.1 0.0 copy-done.2
  146.1 0.1 select_reduce_fusion.1
  146.2 0.7 dynamic_slice.3
  146.9 1.3 subtract_select_fusion
  (6 shorter events, 0.0 us)
Async XLA Ops:
  108.0 20.4 %copy-start = (s32[768]{0:T(1024)S(1)}, s32[768]{0:T(1024)}, u32[]{:S(2)}) copy-start(s32[768]{0:T(1024)} %param.9) | copy-start | bytes 9220
  128.4 17.7 %copy-start.1 = (s32[64]{0:T(128)S(1)}, s32[64]{0:T(128)}, u32[]{:S(2)}) copy-start(s32[64]{0:T(128)} %param.10) | copy-start | bytes 772
  128.4 17.7 %copy-start.2 = (s32[64]{0:T(128)S(1)}, s32[64]{0:T(128)}, u32[]{:S(2)}) copy-start(s32[64]{0:T(128)} %param.11) | copy-start | bytes 772

commit v12 on v11

--- a/solution.py
+++ b/solution.py
@@ -189,7 +189,7 @@
 def gather_all(head, hidden, gain, ny, nz, nv):
     rows, width = head.shape
     slots, breadth = hidden.shape
-    split = max(128, min(width - 128, int(round(width * 0.405 / 128)) * 128))
+    split = max(128, min(width - 128, int(round(width * 0.384 / 128)) * 128))
     streams = 4 * (ny // 2 + nz // 2 + ny * (nz // 2) + nz * (ny // 2))
     out, normed = pl.pallas_call(
         functools.partial(head_gather_kernel, ny, nz, nv, split),

time: 148 us -> 149 us (level)
  no operation moved by 1% of the time
where the time goes in v12:
time: 149 us
  Pallas kernels  115 us (77%)
  matrix products  20.4 us (14%)
  other arithmetic  11.5 us (8%)
    pallas_call x1, Pallas kernels, gather_all(): pl.pallas_call(functools.partial(head_gather_kernel, ny, nz, nv, split),...  106 us
    dot_general x1, matrix products, local(): logits = jnp.dot(normed, columns, preferred_element_type=jnp.float32)  20.4 us
    pallas_call x1, Pallas kernels, exchange_stats(): pl.pallas_call(functools.partial(stats_kernel, n), out_shape=jax.ShapeDty...  9.67 us
    reduce_sum x1, other arithmetic, local(): total_local = jnp.sum(expo, axis=1)  6.99 us

profile of v12, /device:TPU:1, one launch (start us, length us, event | category | flops | bytes accessed | tf_op | source)
XLA Modules:
  0.0 148.8 jit_solution(7449590096905112645)
XLA Ops:
  0.6 1.3 reshape.20
  1.9 105.8 %shard_map.77 = (bf16[4,8,64,4000]{3,2,1,0:T(8,128)(2,1)}, bf16[768,2048]{1,0:T(8,128)(2,1)}) custom-call(bf16[64,4000]{1,0:T(8,128)(2,1)} %head_ref.1, bf16[768,256]{1,0:T(8,128)(2,1)} %hidden_ref.1, f32[1,2048]{1,0:T(1,128)} %bitcast.25), custom_call_target="tpu_custom_call" | custom-call | bytes 32768000 | tf_op jit(solution)/shard_map/pallas_call | solution.py:194
  107.7 0.0 copy-start
  107.8 20.4 %fusion.7 = (f32[768]{0:T(1024)S(1)}, f32[768,4000]{0,1:T(8,128)}) fusion(bf16[768,2048]{1,0:T(8,128)(2,1)} %get-tuple-element.4, bf16[2048,4000]{1,0:T(8,128)(2,1)} %bitcast.26), kind=kOutput, calls=%fused_computation.24 | convolution fusion | flops 12585982976 | bytes 31820800 | tf_op jit(solution)/shard_map/dot_general | solution.py:270
  128.2 0.0 copy-start.1
  128.2 0.0 copy-start.2
  128.2 0.0 copy-done
  128.2 7.0 %fusion = (f32[768]{0:T(1024)S(1)}, f32[768]{0:T(1024)S(1)}, f32[768]{0:T(1024)S(1)}) fusion(f32[768,4000]{0,1:T(8,128)} %get-tuple-element.21, f32[768]{0:T(1024)S(1)} %get-tuple-element.20, s32[768]{0:T(1024)S(1)} %broadcast_subtract_fusion), kind=kLoop, calls=%fused_computation.4 | loop fusion | flops 21501696 | bytes 12303360 | tf_op jit(solution)/shard_map/reduce_sum | solution.py:273
  135.2 0.6 pad_maximum_fusion.stats_ref
  135.8 9.7 %shard_map.78 = f32[8,4,768]{2,1,0:T(4,128)} custom-call(f32[4,768]{1,0:T(4,128)} %pad_maximum_fusion.stats_ref), custom_call_target="tpu_custom_call" | custom-call | tf_op jit(solution)/shard_map/pallas_call | solution.py:246
  145.5 1.2 fusion.6
  146.7 0.0 copy-done.1
  146.8 0.0 copy-done.2
  146.8 0.1 select_reduce_fusion.1
  146.9 0.7 dynamic_slice.3
  147.5 1.3 subtract_select_fusion
  (6 shorter events, 0.0 us)
Async XLA Ops:
  107.7 20.4 %copy-start = (s32[768]{0:T(1024)S(1)}, s32[768]{0:T(1024)}, u32[]{:S(2)}) copy-start(s32[768]{0:T(1024)} %param.9) | copy-start | bytes 9220
  128.2 18.6 %copy-start.1 = (s32[64]{0:T(128)S(1)}, s32[64]{0:T(128)}, u32[]{:S(2)}) copy-start(s32[64]{0:T(128)} %param.10) | copy-start | bytes 772
  128.2 18.6 %copy-start.2 = (s32[64]{0:T(128)S(1)}, s32[64]{0:T(128)}, u32[]{:S(2)}) copy-start(s32[64]{0:T(128)} %param.11) | copy-start | bytes 772

commit v13 on v12

--- a/solution.py
+++ b/solution.py
@@ -97,7 +97,11 @@
             for side, peer, sign in (("r", right, -1), ("l", left, 1)):
                 key = f"{name}{side}{step}"
                 view = block(sign * (step - 1))
-                if 2 * step == n:
+                if 2 * step == n and opp != "split":
+                    if side != opp:
+                        continue
+                    src = first_src if (step == 1 and first_src is not None) else view
+                elif 2 * step == n:
                     view = view.at[pl.ds(0, hr)] if side == "r" else view.at[pl.ds(hr, rows - hr)]
                     src = view
                 elif step == 1 and first_src is not None:
@@ -118,13 +122,14 @@
             return []
         k = abs(offset) if abs(offset) <= steps else n - abs(offset)
         if 2 * k == n:
-            return [f"{name}r{k}", f"{name}l{k}"]
+            return [f"{name}r{k}", f"{name}l{k}"] if opp == "split" else [f"{name}{opp}{k}"]
         return [f"{name}r{k}"] if offset < 0 else [f"{name}l{k}"]
 
     y_offsets = [0] + [s * k for k in range(1, ny // 2 + 1) for s in (-1, 1) if not (s == 1 and 2 * k == ny)]
     z_offsets = [0] + [s * k for k in range(1, nz // 2 + 1) for s in (-1, 1) if not (s == 1 and 2 * k == nz)]
     for q in range(parts):
         rq = pl.ds(q * prow, prow)
+        opp = "r" if q % 2 == 0 else "l"
         ring_plan(f"ay{q}", ny, lambda k: out_ref.at[ys(k), z, rq, cols[0]], right_y, left_y,
                   head_ref.at[rq, cols[0]], [])
         ring_plan(f"bz{q}", nz, lambda k: out_ref.at[y, zs(k), rq, cols[1]], right_z, left_z,

time: 149 us -> 149 us (level)
  no operation moved by 1% of the time
where the time goes in v13:
time: 149 us; the launch traced here: 148 us
  Pallas kernels  115 us (77%)
  matrix products  20.4 us (14%)
  other arithmetic  11.5 us (8%)
    pallas_call x1, Pallas kernels, gather_all(): pl.pallas_call(functools.partial(head_gather_kernel, ny, nz, nv, split),...  106 us
    dot_general x1, matrix products, local(): logits = jnp.dot(normed, columns, preferred_element_type=jnp.float32)  20.4 us
    pallas_call x1, Pallas kernels, exchange_stats(): pl.pallas_call(functools.partial(stats_kernel, n), out_shape=jax.ShapeDty...  9.23 us
    reduce_sum x1, other arithmetic, local(): total_local = jnp.sum(expo, axis=1)  6.99 us

profile of v13, /device:TPU:1, one launch (start us, length us, event | category | flops | bytes accessed | tf_op | source)
XLA Modules:
  0.0 148.3 jit_solution(17878232432907216236)
XLA Ops:
  0.6 1.3 reshape.20
  1.9 105.7 %shard_map.77 = (bf16[4,8,64,4000]{3,2,1,0:T(8,128)(2,1)}, bf16[768,2048]{1,0:T(8,128)(2,1)}) custom-call(bf16[64,4000]{1,0:T(8,128)(2,1)} %head_ref.1, bf16[768,256]{1,0:T(8,128)(2,1)} %hidden_ref.1, f32[1,2048]{1,0:T(1,128)} %bitcast.25), custom_call_target="tpu_custom_call" | custom-call | bytes 32768000 | tf_op jit(solution)/shard_map/pallas_call | solution.py:199
  107.6 0.0 copy-start
  107.6 20.4 %fusion.7 = (f32[768]{0:T(1024)S(1)}, f32[768,4000]{0,1:T(8,128)}) fusion(bf16[768,2048]{1,0:T(8,128)(2,1)} %get-tuple-element.4, bf16[2048,4000]{1,0:T(8,128)(2,1)} %bitcast.26), kind=kOutput, calls=%fused_computation.24 | convolution fusion | flops 12585982976 | bytes 31820800 | tf_op jit(solution)/shard_map/dot_general | solution.py:275
  128.0 0.0 copy-start.1
  128.0 0.0 copy-start.2
  128.0 0.0 copy-done
  128.1 7.0 %fusion = (f32[768]{0:T(1024)S(1)}, f32[768]{0:T(1024)S(1)}, f32[768]{0:T(1024)S(1)}) fusion(f32[768,4000]{0,1:T(8,128)} %get-tuple-element.21, f32[768]{0:T(1024)S(1)} %get-tuple-element.20, s32[768]{0:T(1024)S(1)} %broadcast_subtract_fusion), kind=kLoop, calls=%fused_computation.4 | loop fusion | flops 21501696 | bytes 12303360 | tf_op jit(solution)/shard_map/reduce_sum | solution.py:278
  135.1 0.6 pad_maximum_fusion.stats_ref
  135.7 9.2 %shard_map.78 = f32[8,4,768]{2,1,0:T(4,128)} custom-call(f32[4,768]{1,0:T(4,128)} %pad_maximum_fusion.stats_ref), custom_call_target="tpu_custom_call" | custom-call | tf_op jit(solution)/shard_map/pallas_call | solution.py:251
  145.0 1.2 fusion.6
  146.2 0.0 copy-done.1
  146.2 0.0 copy-done.2
  146.2 0.1 select_reduce_fusion.1
  146.3 0.7 dynamic_slice.3
  147.0 1.3 subtract_select_fusion
  (6 shorter events, 0.0 us)
Async XLA Ops:
  107.6 20.4 %copy-start = (s32[768]{0:T(1024)S(1)}, s32[768]{0:T(1024)}, u32[]{:S(2)}) copy-start(s32[768]{0:T(1024)} %param.9) | copy-start | bytes 9220
  128.0 18.2 %copy-start.1 = (s32[64]{0:T(128)S(1)}, s32[64]{0:T(128)}, u32[]{:S(2)}) copy-start(s32[64]{0:T(128)} %param.10) | copy-start | bytes 772
  128.0 18.2 %copy-start.2 = (s32[64]{0:T(128)S(1)}, s32[64]{0:T(128)}, u32[]{:S(2)}) copy-start(s32[64]{0:T(128)} %param.11) | copy-start | bytes 772

commit v14 on v12

--- a/solution.py
+++ b/solution.py
@@ -273,8 +273,9 @@
     total_local = jnp.sum(expo, axis=1)
     weighted_local = jnp.sum(expo * logits, axis=1)
     local_id = target_ids - slice_index * breadth
-    ids = lax.broadcasted_iota(jnp.int32, logits.shape, 1)
-    picked_local = jnp.sum(jnp.where(ids == local_id[:, None], logits, 0.0), axis=1)
+    inside = (local_id >= 0) & (local_id < breadth)
+    chosen = jnp.take_along_axis(logits, jnp.clip(local_id, 0, breadth - 1)[:, None], axis=1)[:, 0]
+    picked_local = jnp.where(inside, chosen, 0.0)
     stats = jnp.stack([top_local, total_local, weighted_local, picked_local])
     every = exchange_stats(stats, slices)
     tops = every[:, 0]

time: 149 us -> 175 us (1.17)
  local copies, waits for them, and re-layouts: 0.7 us -> 23.6 us
  Pallas kernels: 115 us -> 118 us
    gather x0 -> x1, local copies, waits for them, and re-layouts: none -> 22.9 us  [local(): jnp.take_along_axis(logits, jnp.clip(local_id, 0, breadth - 1)[:, None],...]
    pallas_call x1, Pallas kernels: 9.67 us -> 12.1 us  [exchange_stats(): pl.pallas_call(functools.partial(stats_kernel, n), out_shape=jax.ShapeDty...]
where the time goes in v14:
time: 175 us; the launch traced here: 174 us
  Pallas kernels  118 us (67%)
  local copies, waits for them, and re-layouts  23.6 us (13%)
  matrix products  20.4 us (12%)
  other arithmetic  10.8 us (6%)
    pallas_call x1, Pallas kernels, gather_all(): pl.pallas_call(functools.partial(head_gather_kernel, ny, nz, nv, split),...  106 us
    gather x1, local copies, waits for them, and re-layouts, local(): jnp.take_along_axis(logits, jnp.clip(local_id, 0, breadth - 1)[:, None],...  22.9 us
    dot_general x1, matrix products, local(): logits = jnp.dot(normed, columns, preferred_element_type=jnp.float32)  20.4 us
    pallas_call x1, Pallas kernels, exchange_stats(): pl.pallas_call(functools.partial(stats_kernel, n), out_shape=jax.ShapeDty...  12.1 us
    reduce_sum x1, other arithmetic, local(): total_local = jnp.sum(expo, axis=1)  6.21 us

profile of v14, /device:TPU:1, one launch (start us, length us, event | category | flops | bytes accessed | tf_op | source)
XLA Modules:
  0.0 173.5 jit_solution(4282713163376959594)
XLA Ops:
  0.6 1.3 reshape.42
  1.9 105.8 %shard_map.77 = (bf16[4,8,64,4000]{3,2,1,0:T(8,128)(2,1)}, bf16[768,2048]{1,0:T(8,128)(2,1)}) custom-call(bf16[64,4000]{1,0:T(8,128)(2,1)} %head_ref.1, bf16[768,256]{1,0:T(8,128)(2,1)} %hidden_ref.1, f32[1,2048]{1,0:T(1,128)} %bitcast.27), custom_call_target="tpu_custom_call" | custom-call | bytes 32768000 | tf_op jit(solution)/shard_map/pallas_call | solution.py:194
  107.7 20.4 %fusion.11 = (f32[768]{0:T(1024)S(1)}, f32[768,4000]{0,1:T(8,128)}) fusion(bf16[768,2048]{1,0:T(8,128)(2,1)} %get-tuple-element.4, bf16[2048,4000]{1,0:T(8,128)(2,1)} %bitcast.28), kind=kOutput, calls=%fused_computation.31 | convolution fusion | flops 12585982976 | bytes 31820800 | tf_op jit(solution)/shard_map/dot_general | solution.py:270
  128.1 0.0 copy-start
  128.1 0.0 copy-start.1
  128.1 0.0 copy-start.2
  128.2 6.2 %fusion = (f32[768]{0:T(1024)S(1)}, f32[768]{0:T(1024)S(1)}) fusion(f32[768,4000]{0,1:T(8,128)} %get-tuple-element.20, f32[768]{0:T(1024)S(1)} %get-tuple-element.19), kind=kLoop, calls=%fused_computation.3 | loop fusion | flops 12286464 | bytes 12297216 | tf_op jit(solution)/shard_map/reduce_sum | solution.py:273
  134.4 0.0 copy-done
  134.5 22.9 %gather_fusion = f32[768]{0:T(1024)S(1)} fusion(f32[768,4000]{0,1:T(8,128)} %get-tuple-element.20, s32[768]{0:T(1024)S(1)} %fusion.9), kind=kCustom, calls=%fused_computation | custom fusion | bytes 12288 | tf_op jit(solution)/shard_map/jit(take_along_axis)/gather | solution.py:277
  157.4 0.6 pad_maximum_fusion.stats_ref
  158.0 12.1 %shard_map.78 = f32[8,4,768]{2,1,0:T(4,128)} custom-call(f32[4,768]{1,0:T(4,128)} %pad_maximum_fusion.stats_ref), custom_call_target="tpu_custom_call" | custom-call | tf_op jit(solution)/shard_map/pallas_call | solution.py:246
  170.2 1.2 fusion.10
  171.4 0.0 copy-done.1
  171.4 0.0 copy-done.2
  171.4 0.1 select_reduce_fusion
  171.5 0.7 dynamic_slice.3
  172.2 1.3 subtract_select_fusion
  (11 shorter events, 0.1 us)
Async XLA Ops:
  128.1 6.2 %copy-start = (s32[768]{0:T(1024)S(1)}, s32[768]{0:T(1024)}, u32[]{:S(2)}) copy-start(s32[768]{0:T(1024)} %param.9) | copy-start | bytes 9220
  128.1 43.3 %copy-start.1 = (s32[64]{0:T(128)S(1)}, s32[64]{0:T(128)}, u32[]{:S(2)}) copy-start(s32[64]{0:T(128)} %param.10) | copy-start | bytes 772
  128.1 43.3 %copy-start.2 = (s32[64]{0:T(128)S(1)}, s32[64]{0:T(128)}, u32[]{:S(2)}) copy-start(s32[64]{0:T(128)} %param.11) | copy-start | bytes 772

commit v15 on v12

--- a/solution.py
+++ b/solution.py
@@ -74,20 +74,6 @@
 
     breadth = hidden_ref.shape[1]
     own_cols = feat_ref.at[:, pl.ds(pl.multiple_of(v * breadth, breadth), breadth)]
-    hidden_copies = []
-    for k in range(1, nv):
-        c = pltpu.make_async_remote_copy(
-            src_ref=hidden_ref,
-            dst_ref=own_cols,
-            send_sem=hsend_sem.at[k - 1],
-            recv_sem=hrecv_sem.at[k - 1],
-            device_id=(dp, (v + k) % nv),
-            device_id_type=MESH,
-        )
-        c.start()
-        hidden_copies.append(c)
-    hidden_local = pltpu.make_async_copy(hidden_ref, own_cols, hlocal_sem)
-    hidden_local.start()
 
     plan = []
 
@@ -147,8 +133,24 @@
     index = {plan[i][0]: i for i in range(len(plan))}
     waited = set()
     copies = {}
+    hidden_copies = []
+    hidden_local = None
     for i in order:
         key, src, dst, peer, needs = plan[i]
+        if hidden_local is None and level[key] >= 1:
+            for k in range(1, nv):
+                c = pltpu.make_async_remote_copy(
+                    src_ref=hidden_ref,
+                    dst_ref=own_cols,
+                    send_sem=hsend_sem.at[k - 1],
+                    recv_sem=hrecv_sem.at[k - 1],
+                    device_id=(dp, (v + k) % nv),
+                    device_id_type=MESH,
+                )
+                c.start()
+                hidden_copies.append(c)
+            hidden_local = pltpu.make_async_copy(hidden_ref, own_cols, hlocal_sem)
+            hidden_local.start()
         for n in needs:
             if n not in waited:
                 copies[n].wait_recv()

time: 149 us -> 149 us (level)
  no operation moved by 1% of the time
where the time goes in v15:
time: 149 us
  Pallas kernels  115 us (77%)
  matrix products  20.4 us (14%)
  other arithmetic  11.5 us (8%)
    pallas_call x1, Pallas kernels, gather_all(): pl.pallas_call(functools.partial(head_gather_kernel, ny, nz, nv, split),...  106 us
    dot_general x1, matrix products, local(): logits = jnp.dot(normed, columns, preferred_element_type=jnp.float32)  20.4 us
    pallas_call x1, Pallas kernels, exchange_stats(): pl.pallas_call(functools.partial(stats_kernel, n), out_shape=jax.ShapeDty...  9.67 us
    reduce_sum x1, other arithmetic, local(): total_local = jnp.sum(expo, axis=1)  6.99 us

profile of v15, /device:TPU:1, one launch (start us, length us, event | category | flops | bytes accessed | tf_op | source)
XLA Modules:
  0.0 148.8 jit_solution(10423527355677444408)
XLA Ops:
  0.6 1.3 reshape.20
  1.9 105.8 %shard_map.77 = (bf16[4,8,64,4000]{3,2,1,0:T(8,128)(2,1)}, bf16[768,2048]{1,0:T(8,128)(2,1)}) custom-call(bf16[64,4000]{1,0:T(8,128)(2,1)} %head_ref.1, bf16[768,256]{1,0:T(8,128)(2,1)} %hidden_ref.1, f32[1,2048]{1,0:T(1,128)} %bitcast.25), custom_call_target="tpu_custom_call" | custom-call | bytes 32768000 | tf_op jit(solution)/shard_map/pallas_call | solution.py:196
  107.7 0.0 copy-start
  107.8 20.4 %fusion.7 = (f32[768]{0:T(1024)S(1)}, f32[768,4000]{0,1:T(8,128)}) fusion(bf16[768,2048]{1,0:T(8,128)(2,1)} %get-tuple-element.4, bf16[2048,4000]{1,0:T(8,128)(2,1)} %bitcast.26), kind=kOutput, calls=%fused_computation.24 | convolution fusion | flops 12585982976 | bytes 31820800 | tf_op jit(solution)/shard_map/dot_general | solution.py:272
  128.2 0.0 copy-start.1
  128.2 0.0 copy-start.2
  128.2 0.0 copy-done
  128.2 7.0 %fusion = (f32[768]{0:T(1024)S(1)}, f32[768]{0:T(1024)S(1)}, f32[768]{0:T(1024)S(1)}) fusion(f32[768,4000]{0,1:T(8,128)} %get-tuple-element.21, f32[768]{0:T(1024)S(1)} %get-tuple-element.20, s32[768]{0:T(1024)S(1)} %broadcast_subtract_fusion), kind=kLoop, calls=%fused_computation.4 | loop fusion | flops 21501696 | bytes 12303360 | tf_op jit(solution)/shard_map/reduce_sum | solution.py:275
  135.2 0.6 pad_maximum_fusion.stats_ref
  135.8 9.7 %shard_map.78 = f32[8,4,768]{2,1,0:T(4,128)} custom-call(f32[4,768]{1,0:T(4,128)} %pad_maximum_fusion.stats_ref), custom_call_target="tpu_custom_call" | custom-call | tf_op jit(solution)/shard_map/pallas_call | solution.py:248
  145.5 1.2 fusion.6
  146.7 0.0 copy-done.1
  146.8 0.0 copy-done.2
  146.8 0.1 select_reduce_fusion.1
  146.9 0.7 dynamic_slice.3
  147.5 1.3 subtract_select_fusion
  (6 shorter events, 0.0 us)
Async XLA Ops:
  107.7 20.4 %copy-start = (s32[768]{0:T(1024)S(1)}, s32[768]{0:T(1024)}, u32[]{:S(2)}) copy-start(s32[768]{0:T(1024)} %param.9) | copy-start | bytes 9220
  128.2 18.6 %copy-start.1 = (s32[64]{0:T(128)S(1)}, s32[64]{0:T(128)}, u32[]{:S(2)}) copy-start(s32[64]{0:T(128)} %param.10) | copy-start | bytes 772
  128.2 18.6 %copy-start.2 = (s32[64]{0:T(128)S(1)}, s32[64]{0:T(128)}, u32[]{:S(2)}) copy-start(s32[64]{0:T(128)} %param.11) | copy-start | bytes 772

commit v16 on v12

--- a/solution.py
+++ b/solution.py
@@ -189,7 +189,7 @@
 def gather_all(head, hidden, gain, ny, nz, nv):
     rows, width = head.shape
     slots, breadth = hidden.shape
-    split = max(128, min(width - 128, int(round(width * 0.384 / 128)) * 128))
+    split = max(128, min(width - 128, int(round(width * 0.45 / 128)) * 128))
     streams = 4 * (ny // 2 + nz // 2 + ny * (nz // 2) + nz * (ny // 2))
     out, normed = pl.pallas_call(
         functools.partial(head_gather_kernel, ny, nz, nv, split),

time: 149 us -> 152 us (1.020)
  Pallas kernels: 115 us -> 118 us
    pallas_call x1, Pallas kernels: 106 us -> 110 us  [gather_all(): pl.pallas_call(functools.partial(head_gather_kernel, ny, nz, nv, split),...]
where the time goes in v16:
time: 152 us
  Pallas kernels  118 us (78%)
  matrix products  20.4 us (13%)
  other arithmetic  11.5 us (8%)
    pallas_call x1, Pallas kernels, gather_all(): pl.pallas_call(functools.partial(head_gather_kernel, ny, nz, nv, split),...  110 us
    dot_general x1, matrix products, local(): logits = jnp.dot(normed, columns, preferred_element_type=jnp.float32)  20.4 us
    pallas_call x1, Pallas kernels, exchange_stats(): pl.pallas_call(functools.partial(stats_kernel, n), out_shape=jax.ShapeDty...  8.75 us
    reduce_sum x1, other arithmetic, local(): total_local = jnp.sum(expo, axis=1)  6.99 us

profile of v16, /device:TPU:1, one launch (start us, length us, event | category | flops | bytes accessed | tf_op | source)
XLA Modules:
  0.0 151.7 jit_solution(2339057534654719108)
XLA Ops:
  0.6 1.3 reshape.20
  1.9 109.6 %shard_map.77 = (bf16[4,8,64,4000]{3,2,1,0:T(8,128)(2,1)}, bf16[768,2048]{1,0:T(8,128)(2,1)}) custom-call(bf16[64,4000]{1,0:T(8,128)(2,1)} %head_ref.1, bf16[768,256]{1,0:T(8,128)(2,1)} %hidden_ref.1, f32[1,2048]{1,0:T(1,128)} %bitcast.25), custom_call_target="tpu_custom_call" | custom-call | bytes 32768000 | tf_op jit(solution)/shard_map/pallas_call | solution.py:194
  111.5 0.0 copy-start
  111.5 20.4 %fusion.7 = (f32[768]{0:T(1024)S(1)}, f32[768,4000]{0,1:T(8,128)}) fusion(bf16[768,2048]{1,0:T(8,128)(2,1)} %get-tuple-element.4, bf16[2048,4000]{1,0:T(8,128)(2,1)} %bitcast.26), kind=kOutput, calls=%fused_computation.24 | convolution fusion | flops 12585982976 | bytes 31820800 | tf_op jit(solution)/shard_map/dot_general | solution.py:270
  131.9 0.0 copy-start.1
  131.9 0.0 copy-start.2
  131.9 0.0 copy-done
  131.9 7.0 %fusion = (f32[768]{0:T(1024)S(1)}, f32[768]{0:T(1024)S(1)}, f32[768]{0:T(1024)S(1)}) fusion(f32[768,4000]{0,1:T(8,128)} %get-tuple-element.21, f32[768]{0:T(1024)S(1)} %get-tuple-element.20, s32[768]{0:T(1024)S(1)} %broadcast_subtract_fusion), kind=kLoop, calls=%fused_computation.4 | loop fusion | flops 21501696 | bytes 12303360 | tf_op jit(solution)/shard_map/reduce_sum | solution.py:273
  139.0 0.6 pad_maximum_fusion.stats_ref
  139.6 8.7 %shard_map.78 = f32[8,4,768]{2,1,0:T(4,128)} custom-call(f32[4,768]{1,0:T(4,128)} %pad_maximum_fusion.stats_ref), custom_call_target="tpu_custom_call" | custom-call | tf_op jit(solution)/shard_map/pallas_call | solution.py:246
  148.3 1.2 fusion.6
  149.6 0.0 copy-done.1
  149.6 0.0 copy-done.2
  149.6 0.1 select_reduce_fusion.1
  149.7 0.7 dynamic_slice.3
  150.4 1.3 subtract_select_fusion
  (6 shorter events, 0.0 us)
Async XLA Ops:
  111.5 20.4 %copy-start = (s32[768]{0:T(1024)S(1)}, s32[768]{0:T(1024)}, u32[]{:S(2)}) copy-start(s32[768]{0:T(1024)} %param.9) | copy-start | bytes 9220
  131.9 17.7 %copy-start.1 = (s32[64]{0:T(128)S(1)}, s32[64]{0:T(128)}, u32[]{:S(2)}) copy-start(s32[64]{0:T(128)} %param.10) | copy-start | bytes 772
  131.9 17.7 %copy-start.2 = (s32[64]{0:T(128)S(1)}, s32[64]{0:T(128)}, u32[]{:S(2)}) copy-start(s32[64]{0:T(128)} %param.11) | copy-start | bytes 772

commit v17 on v12

--- a/solution.py
+++ b/solution.py
@@ -143,7 +143,11 @@
     level = {}
     for key, _, _, _, needs in plan:
         level[key] = 1 + max([level[n] for n in needs], default=-1)
-    order = sorted(range(len(plan)), key=lambda i: (level[plan[i][0]], i))
+    tail = {key: 0 for key, _, _, _, _ in plan}
+    for key, _, _, _, needs in reversed(plan):
+        for n in needs:
+            tail[n] = max(tail[n], tail[key] + 1)
+    order = sorted(range(len(plan)), key=lambda i: (level[plan[i][0]], -tail[plan[i][0]], i))
     index = {plan[i][0]: i for i in range(len(plan))}
     waited = set()
     copies = {}

time: 149 us -> 150 us (level)
    pallas_call x1, Pallas kernels: 106 us -> 107 us  [gather_all(): pl.pallas_call(functools.partial(head_gather_kernel, ny, nz, nv, split),...]
where the time goes in v17:
time: 150 us; the launch traced here: 149 us
  Pallas kernels  116 us (77%)
  matrix products  20.4 us (14%)
  other arithmetic  11.5 us (8%)
    pallas_call x1, Pallas kernels, gather_all(): pl.pallas_call(functools.partial(head_gather_kernel, ny, nz, nv, split),...  107 us
    dot_general x1, matrix products, local(): logits = jnp.dot(normed, columns, preferred_element_type=jnp.float32)  20.4 us
    pallas_call x1, Pallas kernels, exchange_stats(): pl.pallas_call(functools.partial(stats_kernel, n), out_shape=jax.ShapeDty...  8.52 us
    reduce_sum x1, other arithmetic, local(): total_local = jnp.sum(expo, axis=1)  6.99 us

profile of v17, /device:TPU:1, one launch (start us, length us, event | category | flops | bytes accessed | tf_op | source)
XLA Modules:
  0.0 149.4 jit_solution(16589917457073714006)
XLA Ops:
  0.6 1.3 reshape.20
  1.9 107.5 %shard_map.77 = (bf16[4,8,64,4000]{3,2,1,0:T(8,128)(2,1)}, bf16[768,2048]{1,0:T(8,128)(2,1)}) custom-call(bf16[64,4000]{1,0:T(8,128)(2,1)} %head_ref.1, bf16[768,256]{1,0:T(8,128)(2,1)} %hidden_ref.1, f32[1,2048]{1,0:T(1,128)} %bitcast.25), custom_call_target="tpu_custom_call" | custom-call | bytes 32768000 | tf_op jit(solution)/shard_map/pallas_call | solution.py:198
  109.4 0.0 copy-start
  109.4 20.4 %fusion.7 = (f32[768]{0:T(1024)S(1)}, f32[768,4000]{0,1:T(8,128)}) fusion(bf16[768,2048]{1,0:T(8,128)(2,1)} %get-tuple-element.4, bf16[2048,4000]{1,0:T(8,128)(2,1)} %bitcast.26), kind=kOutput, calls=%fused_computation.24 | convolution fusion | flops 12585982976 | bytes 31820800 | tf_op jit(solution)/shard_map/dot_general | solution.py:274
  129.8 0.0 copy-start.1
  129.8 0.0 copy-start.2
  129.8 0.0 copy-done
  129.8 7.0 %fusion = (f32[768]{0:T(1024)S(1)}, f32[768]{0:T(1024)S(1)}, f32[768]{0:T(1024)S(1)}) fusion(f32[768,4000]{0,1:T(8,128)} %get-tuple-element.21, f32[768]{0:T(1024)S(1)} %get-tuple-element.20, s32[768]{0:T(1024)S(1)} %broadcast_subtract_fusion), kind=kLoop, calls=%fused_computation.4 | loop fusion | flops 21501696 | bytes 12303360 | tf_op jit(solution)/shard_map/reduce_sum | solution.py:277
  136.9 0.6 pad_maximum_fusion.stats_ref
  137.5 8.5 %shard_map.78 = f32[8,4,768]{2,1,0:T(4,128)} custom-call(f32[4,768]{1,0:T(4,128)} %pad_maximum_fusion.stats_ref), custom_call_target="tpu_custom_call" | custom-call | tf_op jit(solution)/shard_map/pallas_call | solution.py:250
  146.0 1.2 fusion.6
  147.3 0.0 copy-done.1
  147.3 0.0 copy-done.2
  147.3 0.1 select_reduce_fusion.1
  147.4 0.7 dynamic_slice.3
  148.1 1.3 subtract_select_fusion
  (6 shorter events, 0.0 us)
Async XLA Ops:
  109.4 20.4 %copy-start = (s32[768]{0:T(1024)S(1)}, s32[768]{0:T(1024)}, u32[]{:S(2)}) copy-start(s32[768]{0:T(1024)} %param.9) | copy-start | bytes 9220
  129.8 17.4 %copy-start.1 = (s32[64]{0:T(128)S(1)}, s32[64]{0:T(128)}, u32[]{:S(2)}) copy-start(s32[64]{0:T(128)} %param.10) | copy-start | bytes 772
  129.8 17.5 %copy-start.2 = (s32[64]{0:T(128)S(1)}, s32[64]{0:T(128)}, u32[]{:S(2)}) copy-start(s32[64]{0:T(128)} %param.11) | copy-start | bytes 772

commit v18 on v12

--- a/solution.py
+++ b/solution.py
@@ -166,7 +166,7 @@
     hidden_local.wait()
     for c in hidden_copies:
         c.wait_recv()
-    tile = 64
+    tile = 256
 
     def norm_rows(i, carry):
         r = pl.ds(pl.multiple_of(i * tile, tile), tile)

time: 149 us -> 149 us (level)
  no operation moved by 1% of the time
where the time goes in v18:
time: 149 us
  Pallas kernels  115 us (77%)
  matrix products  20.4 us (14%)
  other arithmetic  11.5 us (8%)
    pallas_call x1, Pallas kernels, gather_all(): pl.pallas_call(functools.partial(head_gather_kernel, ny, nz, nv, split),...  106 us
    dot_general x1, matrix products, local(): logits = jnp.dot(normed, columns, preferred_element_type=jnp.float32)  20.4 us
    pallas_call x1, Pallas kernels, exchange_stats(): pl.pallas_call(functools.partial(stats_kernel, n), out_shape=jax.ShapeDty...  9.67 us
    reduce_sum x1, other arithmetic, local(): total_local = jnp.sum(expo, axis=1)  6.99 us

profile of v18, /device:TPU:1, one launch (start us, length us, event | category | flops | bytes accessed | tf_op | source)
XLA Modules:
  0.0 148.8 jit_solution(15497137872794360268)
XLA Ops:
  0.6 1.3 reshape.20
  1.9 105.8 %shard_map.77 = (bf16[4,8,64,4000]{3,2,1,0:T(8,128)(2,1)}, bf16[768,2048]{1,0:T(8,128)(2,1)}) custom-call(bf16[64,4000]{1,0:T(8,128)(2,1)} %head_ref.1, bf16[768,256]{1,0:T(8,128)(2,1)} %hidden_ref.1, f32[1,2048]{1,0:T(1,128)} %bitcast.25), custom_call_target="tpu_custom_call" | custom-call | bytes 32768000 | tf_op jit(solution)/shard_map/pallas_call | solution.py:194
  107.7 0.0 copy-start
  107.8 20.4 %fusion.7 = (f32[768]{0:T(1024)S(1)}, f32[768,4000]{0,1:T(8,128)}) fusion(bf16[768,2048]{1,0:T(8,128)(2,1)} %get-tuple-element.4, bf16[2048,4000]{1,0:T(8,128)(2,1)} %bitcast.26), kind=kOutput, calls=%fused_computation.24 | convolution fusion | flops 12585982976 | bytes 31820800 | tf_op jit(solution)/shard_map/dot_general | solution.py:270
  128.2 0.0 copy-start.1
  128.2 0.0 copy-start.2
  128.2 0.0 copy-done
  128.2 7.0 %fusion = (f32[768]{0:T(1024)S(1)}, f32[768]{0:T(1024)S(1)}, f32[768]{0:T(1024)S(1)}) fusion(f32[768,4000]{0,1:T(8,128)} %get-tuple-element.21, f32[768]{0:T(1024)S(1)} %get-tuple-element.20, s32[768]{0:T(1024)S(1)} %broadcast_subtract_fusion), kind=kLoop, calls=%fused_computation.4 | loop fusion | flops 21501696 | bytes 12303360 | tf_op jit(solution)/shard_map/reduce_sum | solution.py:273
  135.2 0.6 pad_maximum_fusion.stats_ref
  135.8 9.7 %shard_map.78 = f32[8,4,768]{2,1,0:T(4,128)} custom-call(f32[4,768]{1,0:T(4,128)} %pad_maximum_fusion.stats_ref), custom_call_target="tpu_custom_call" | custom-call | tf_op jit(solution)/shard_map/pallas_call | solution.py:246
  145.5 1.2 fusion.6
  146.7 0.0 copy-done.1
  146.8 0.0 copy-done.2
  146.8 0.1 select_reduce_fusion.1
  146.9 0.7 dynamic_slice.3
  147.5 1.3 subtract_select_fusion
  (6 shorter events, 0.0 us)
Async XLA Ops:
  107.7 20.4 %copy-start = (s32[768]{0:T(1024)S(1)}, s32[768]{0:T(1024)}, u32[]{:S(2)}) copy-start(s32[768]{0:T(1024)} %param.9) | copy-start | bytes 9220
  128.2 18.6 %copy-start.1 = (s32[64]{0:T(128)S(1)}, s32[64]{0:T(128)}, u32[]{:S(2)}) copy-start(s32[64]{0:T(128)} %param.10) | copy-start | bytes 772
  128.2 18.6 %copy-start.2 = (s32[64]{0:T(128)S(1)}, s32[64]{0:T(128)}, u32[]{:S(2)}) copy-start(s32[64]{0:T(128)} %param.11) | copy-start | bytes 772
